TPU v7x, 128 devices: a whole 4x4x4 slice. The times are simulated.
128 devices in a mesh: ctx: 16 (over y, x_hi, core), exp: 8 (over x_lo, z).
Axes of the slice: x: 4 (x_hi: 2, x_lo: 2; x = x_hi * 2 + x_lo), y: 4, z: 4, core: 2. Of those that a mesh axis runs over, the one named last changes fastest.
Arguments:
- stream: bfloat16 [2048, 4096], P(('ctx', 'exp')), may hold values from -3 to 3
- queries: bfloat16 [2048, 4096], P('ctx', 'exp'), may hold values from -108 to 108
- attn_keys: bfloat16 [2048, 1024], P('ctx', 'exp'), may hold values from -3 to 3
- attn_values: bfloat16 [2048, 1024], P('ctx', 'exp'), may hold values from -6 to 6
- out_weight: bfloat16 [4096, 4096], P('exp'), may hold values from -0.09375 to 0.09375
- norm_gain: float32 [4096], replicated, may hold values from 0.25 to 1.75
- expert_ids: int32 [2048, 2], P(('ctx', 'exp')), may hold values from 0 to 7, all different within a row; in each aligned block of 16 rows (0 to 15, 16 to 31, ...) at most 8 rows name the same one
- combine: float32 [2048, 2], P(('ctx', 'exp')), may hold values from 0.1 to 0.9
- w_gate: bfloat16 [8, 4096, 14336], P('exp', None, 'ctx'), may hold values from -0.09375 to 0.09375
- w_up: bfloat16 [8, 4096, 14336], P('exp', None, 'ctx'), may hold values from -0.09375 to 0.09375
- w_down: bfloat16 [8, 14336, 4096], P('exp', 'ctx'), may hold values from -0.046875 to 0.046875
Outputs:
- layer_out: bfloat16 [2048, 4096], P(('ctx', 'exp'))
Inputs may be any that keep to these rules, and one draw needn't show every extreme that they name: `expert_ids`: taking the rows in aligned blocks of 16 (the rows of one device), no expert is named by more than 8 rows of a block, and in every draw some block names some expert exactly 8 times. The 2 experts of a row differ.
All inputs are finite; a program needn't handle non-finite values.
Results may differ from a plain program's by a relative error of at most 0.015.
Values may be sent and summed in bfloat16 or wider, within the bound.
A program may use at most 128 MiB of HBM per device.

v0:
```python
import math

import jax
import jax.numpy as jnp
from jax import lax
from jax.sharding import PartitionSpec as P

HEAD_DIM = 128
TOP = 2
GROUP = 4


neg_big = -1e30


def passed_along(block, axis, distance):
    devices = range(lax.axis_size(axis))
    route = [(i - distance, i) for i in devices if i - distance in devices]
    return lax.ppermute(block, axis, route)


def absorb_block(carried, kv_block, key_first, queries_grid, query_pos):
    run_max, run_total, run_acc = carried
    key_rows = kv_block.shape[1]
    kv_heads_dev = queries_grid.shape[1]
    key_block = kv_block[0].reshape(key_rows, kv_heads_dev, HEAD_DIM)
    value_block = kv_block[1].reshape(key_rows, kv_heads_dev, HEAD_DIM)
    scores = jnp.einsum(
        "tkgd,ukd->kgtu", queries_grid, key_block, preferred_element_type=jnp.float32
    ) * (1.0 / math.sqrt(HEAD_DIM))
    key_pos = key_first + jnp.arange(key_rows, dtype=jnp.int32)
    allowed = query_pos[:, None] >= key_pos[None, :]
    scores = jnp.where(allowed, scores, neg_big)
    new_max = jnp.maximum(run_max, jnp.max(scores, axis=-1))
    rescale = jnp.exp(run_max - new_max)
    weights = jnp.where(allowed, jnp.exp(scores - new_max[..., None]), 0.0)
    new_total = run_total * rescale + jnp.sum(weights, axis=-1)
    contrib = jnp.einsum(
        "kgtu,ukd->tkgd",
        weights.astype(jnp.bfloat16),
        value_block,
        preferred_element_type=jnp.float32,
    )
    new_acc = run_acc * jnp.transpose(rescale, (2, 0, 1))[..., None] + contrib
    return (new_max, new_total, new_acc)


def rms_norm(values_f32, norm_gain):
    mean_square = jnp.mean(values_f32 * values_f32, axis=-1, keepdims=True)
    return (values_f32 * lax.rsqrt(mean_square + 1e-05) * norm_gain).astype(jnp.bfloat16)


def slot_table(expert_ids, n_exp, capacity):
    flat_ids = expert_ids.reshape(-1)
    onehot = (flat_ids[:, None] == jnp.arange(n_exp, dtype=jnp.int32)[None, :]).astype(jnp.int32)
    before = jnp.cumsum(onehot, axis=0) - onehot
    slot_rank = jnp.sum(before * onehot, axis=1)
    return flat_ids * capacity + slot_rank


def pick_rows(slot_index, token_count, n_slots, normed):
    chosen = slot_index[None, :] == jnp.arange(n_slots, dtype=jnp.int32)[:, None]
    chosen = jnp.sum(chosen.reshape(n_slots, token_count, TOP).astype(jnp.float32), axis=2)
    return jnp.dot(chosen.astype(jnp.bfloat16), normed, preferred_element_type=jnp.float32).astype(
        jnp.bfloat16
    )


def body(
    stream,
    queries,
    attn_keys,
    attn_values,
    out_weight,
    norm_gain,
    expert_ids,
    combine,
    w_gate,
    w_up,
    w_down,
):
    span = queries.shape[0]
    n_ctx = lax.axis_size("ctx")
    n_exp = lax.axis_size("exp")
    ctx_pos = lax.axis_index("ctx")
    tok_rows = stream.shape[0]
    model_dim = stream.shape[1]
    capacity = max(2, 4 * span // (n_exp * n_exp))
    n_slots = n_exp * capacity
    kv_heads_dev = attn_keys.shape[1] // HEAD_DIM
    queries_grid = queries.reshape(span, kv_heads_dev, GROUP, HEAD_DIM)
    query_pos = ctx_pos * span + jnp.arange(span, dtype=jnp.int32)
    kv_pair = jnp.stack([attn_keys, attn_values])
    start_carry = (
        jnp.full((kv_heads_dev, GROUP, span), neg_big, jnp.float32),
        jnp.zeros((kv_heads_dev, GROUP, span), jnp.float32),
        jnp.zeros((span, kv_heads_dev, GROUP, HEAD_DIM), jnp.float32),
    )
    carried = absorb_block(start_carry, kv_pair, ctx_pos * span, queries_grid, query_pos)

    def advance(turn_index, loop_carry):
        carried_in, travelling = loop_carry
        travelling = passed_along(travelling, "ctx", 1)
        source = ctx_pos - turn_index
        carried_in = lax.cond(
            source >= 0,
            lambda inner_state: absorb_block(
                inner_state, travelling, source * span, queries_grid, query_pos
            ),
            lambda inner_state: inner_state,
            carried_in,
        )
        return (carried_in, travelling)

    carried, final_pair = lax.fori_loop(1, n_ctx, advance, (carried, kv_pair))
    run_max, run_total, run_acc = carried
    attention = (
        (run_acc / jnp.transpose(run_total, (2, 0, 1))[..., None])
        .reshape(span, kv_heads_dev * GROUP * HEAD_DIM)
        .astype(jnp.bfloat16)
    )
    slot_index = slot_table(expert_ids, n_exp, capacity)
    mixed = stream.astype(jnp.float32) + lax.psum_scatter(
        jnp.dot(attention, out_weight, preferred_element_type=jnp.float32).astype(jnp.bfloat16),
        "exp",
        scatter_dimension=0,
        tiled=True,
    ).astype(jnp.float32)
    normed = rms_norm(mixed, norm_gain)
    outgoing = pick_rows(slot_index, tok_rows, n_slots, normed)
    rows_in = lax.all_to_all(
        outgoing.reshape(n_exp, capacity, model_dim), "exp", split_axis=0, concat_axis=0, tiled=True
    ).reshape(n_slots, model_dim)
    gate_mat = w_gate[0]
    up_mat = w_up[0]
    down_mat = w_down[0]
    row_piece = lax.all_gather(rows_in, "ctx", axis=0, tiled=True)
    gate_part = jnp.dot(row_piece, gate_mat, preferred_element_type=jnp.float32)
    up_part = jnp.dot(row_piece, up_mat, preferred_element_type=jnp.float32)
    hidden_all = (jax.nn.silu(gate_part) * up_part).astype(jnp.bfloat16)
    expert_result = lax.psum_scatter(
        jnp.dot(hidden_all, down_mat, preferred_element_type=jnp.float32).astype(jnp.bfloat16),
        "ctx",
        scatter_dimension=0,
        tiled=True,
    )
    returned = lax.all_to_all(
        expert_result.reshape(n_exp, capacity, model_dim),
        "exp",
        split_axis=0,
        concat_axis=0,
        tiled=True,
    ).reshape(n_slots, model_dim)
    picked = (
        jnp.take(returned, slot_index, axis=0).reshape(tok_rows, TOP, model_dim).astype(jnp.float32)
    )
    layer_out = (mixed + jnp.sum(combine[..., None] * picked, axis=1)).astype(jnp.bfloat16)
    return layer_out


def solution(mesh):
    in_specs = (
        P(("ctx", "exp"), None),
        P("ctx", "exp"),
        P("ctx", "exp"),
        P("ctx", "exp"),
        P("exp", None),
        P(),
        P(("ctx", "exp"), None),
        P(("ctx", "exp"), None),
        P("exp", None, "ctx"),
        P("exp", None, "ctx"),
        P("exp", "ctx", None),
    )
    out_specs = P(("ctx", "exp"), None)
    return jax.shard_map(body, mesh=mesh, in_specs=in_specs, out_specs=out_specs, check_vma=False)
```

profile of v0, /device:TPU:29, one launch (start us, length us, event | category | flops | bytes accessed | tf_op | source)
XLA Modules:
  0.0 422.7 jit_solution(11051231305012032276)
XLA Ops:
  10.8 117.6 %while.20 = (s32[]{:T(128)}, f32[1,4,128]{2,1,0:T(4,128)S(1)}, f32[1,4,128]{2,1,0:T(4,128)S(1)}, f32[128,1,4,128]{3,0,2,1:T(8,128)S(1)}, bf16[2,128,128]{2,1,0:T...) while((s32[]{:T(128)}, f32[1,4,128]{2,1,0:T(4,128)S(1)}, ...), condition=%wide.region_7.8_spmd.clone, body=%wide.region_2.7_spmd.clone.sunk | while | flops 34293508 | bytes 2002227 | solution.py:115
  10.9 1.4 collective-permute-start
  12.3 2.0 collective-permute-done
  15.1 1.3 collective-permute-start
  16.4 5.8 %collective-permute-done = bf16[2,128,128]{2,1,0:T(8,128)(2,1)S(1)} collective-permute-done((bf16[2,128,128]{2,1,0:T(8,128)(2,1)S(1)}, bf16[2,128,128]{2,1,0:T(8,128)(2,1)S(1)}, u32[]{:S(2)}, u32[]{:S(2)}) %collective-permute-start) | collective-permute-done | bytes 65568 | tf_op jit(solution)/shard_map/while/body/eval_jaxpr/ppermute | solution.py:19
  22.9 1.3 collective-permute-start
  24.2 5.8 %collective-permute-done = bf16[2,128,128]{2,1,0:T(8,128)(2,1)S(1)} collective-permute-done((bf16[2,128,128]{2,1,0:T(8,128)(2,1)S(1)}, bf16[2,128,128]{2,1,0:T(8,128)(2,1)S(1)}, u32[]{:S(2)}, u32[]{:S(2)}) %collective-permute-start) | collective-permute-done | bytes 65568 | tf_op jit(solution)/shard_map/while/body/eval_jaxpr/ppermute | solution.py:19
  30.7 1.3 collective-permute-start
  32.0 5.8 %collective-permute-done = bf16[2,128,128]{2,1,0:T(8,128)(2,1)S(1)} collective-permute-done((bf16[2,128,128]{2,1,0:T(8,128)(2,1)S(1)}, bf16[2,128,128]{2,1,0:T(8,128)(2,1)S(1)}, u32[]{:S(2)}, u32[]{:S(2)}) %collective-permute-start) | collective-permute-done | bytes 65568 | tf_op jit(solution)/shard_map/while/body/eval_jaxpr/ppermute | solution.py:19
  38.6 1.3 collective-permute-start
  39.9 5.8 %collective-permute-done = bf16[2,128,128]{2,1,0:T(8,128)(2,1)S(1)} collective-permute-done((bf16[2,128,128]{2,1,0:T(8,128)(2,1)S(1)}, bf16[2,128,128]{2,1,0:T(8,128)(2,1)S(1)}, u32[]{:S(2)}, u32[]{:S(2)}) %collective-permute-start) | collective-permute-done | bytes 65568 | tf_op jit(solution)/shard_map/while/body/eval_jaxpr/ppermute | solution.py:19
  47.7 5.8 %collective-permute-done = bf16[2,128,128]{2,1,0:T(8,128)(2,1)S(1)} collective-permute-done((bf16[2,128,128]{2,1,0:T(8,128)(2,1)S(1)}, bf16[2,128,128]{2,1,0:T(8,128)(2,1)S(1)}, u32[]{:S(2)}, u32[]{:S(2)}) %collective-permute-start) | collective-permute-done | bytes 65568 | tf_op jit(solution)/shard_map/while/body/eval_jaxpr/ppermute | solution.py:19
  55.5 5.8 %collective-permute-done = bf16[2,128,128]{2,1,0:T(8,128)(2,1)S(1)} collective-permute-done((bf16[2,128,128]{2,1,0:T(8,128)(2,1)S(1)}, bf16[2,128,128]{2,1,0:T(8,128)(2,1)S(1)}, u32[]{:S(2)}, u32[]{:S(2)}) %collective-permute-start) | collective-permute-done | bytes 65568 | tf_op jit(solution)/shard_map/while/body/eval_jaxpr/ppermute | solution.py:19
  63.4 5.8 %collective-permute-done = bf16[2,128,128]{2,1,0:T(8,128)(2,1)S(1)} collective-permute-done((bf16[2,128,128]{2,1,0:T(8,128)(2,1)S(1)}, bf16[2,128,128]{2,1,0:T(8,128)(2,1)S(1)}, u32[]{:S(2)}, u32[]{:S(2)}) %collective-permute-start) | collective-permute-done | bytes 65568 | tf_op jit(solution)/shard_map/while/body/eval_jaxpr/ppermute | solution.py:19
  71.2 5.8 %collective-permute-done = bf16[2,128,128]{2,1,0:T(8,128)(2,1)S(1)} collective-permute-done((bf16[2,128,128]{2,1,0:T(8,128)(2,1)S(1)}, bf16[2,128,128]{2,1,0:T(8,128)(2,1)S(1)}, u32[]{:S(2)}, u32[]{:S(2)}) %collective-permute-start) | collective-permute-done | bytes 65568 | tf_op jit(solution)/shard_map/while/body/eval_jaxpr/ppermute | solution.py:19
  79.0 5.8 %collective-permute-done = bf16[2,128,128]{2,1,0:T(8,128)(2,1)S(1)} collective-permute-done((bf16[2,128,128]{2,1,0:T(8,128)(2,1)S(1)}, bf16[2,128,128]{2,1,0:T(8,128)(2,1)S(1)}, u32[]{:S(2)}, u32[]{:S(2)}) %collective-permute-start) | collective-permute-done | bytes 65568 | tf_op jit(solution)/shard_map/while/body/eval_jaxpr/ppermute | solution.py:19
  86.9 5.9 %collective-permute-done = bf16[2,128,128]{2,1,0:T(8,128)(2,1)S(1)} collective-permute-done((bf16[2,128,128]{2,1,0:T(8,128)(2,1)S(1)}, bf16[2,128,128]{2,1,0:T(8,128)(2,1)S(1)}, u32[]{:S(2)}, u32[]{:S(2)}) %collective-permute-start) | collective-permute-done | bytes 65568 | tf_op jit(solution)/shard_map/while/body/eval_jaxpr/ppermute | solution.py:19
  94.8 6.7 %collective-permute-done = bf16[2,128,128]{2,1,0:T(8,128)(2,1)S(1)} collective-permute-done((bf16[2,128,128]{2,1,0:T(8,128)(2,1)S(1)}, bf16[2,128,128]{2,1,0:T(8,128)(2,1)S(1)}, u32[]{:S(2)}, u32[]{:S(2)}) %collective-permute-start) | collective-permute-done | bytes 65568 | tf_op jit(solution)/shard_map/while/body/eval_jaxpr/ppermute | solution.py:19
  103.6 6.7 %collective-permute-done = bf16[2,128,128]{2,1,0:T(8,128)(2,1)S(1)} collective-permute-done((bf16[2,128,128]{2,1,0:T(8,128)(2,1)S(1)}, bf16[2,128,128]{2,1,0:T(8,128)(2,1)S(1)}, u32[]{:S(2)}, u32[]{:S(2)}) %collective-permute-start) | collective-permute-done | bytes 65568 | tf_op jit(solution)/shard_map/while/body/eval_jaxpr/ppermute | solution.py:19
  112.3 6.7 %collective-permute-done = bf16[2,128,128]{2,1,0:T(8,128)(2,1)S(1)} collective-permute-done((bf16[2,128,128]{2,1,0:T(8,128)(2,1)S(1)}, bf16[2,128,128]{2,1,0:T(8,128)(2,1)S(1)}, u32[]{:S(2)}, u32[]{:S(2)}) %collective-permute-start) | collective-permute-done | bytes 65568 | tf_op jit(solution)/shard_map/while/body/eval_jaxpr/ppermute | solution.py:19
  119.7 1.3 collective-permute-start
  121.0 6.7 %collective-permute-done = bf16[2,128,128]{2,1,0:T(8,128)(2,1)S(1)} collective-permute-done((bf16[2,128,128]{2,1,0:T(8,128)(2,1)S(1)}, bf16[2,128,128]{2,1,0:T(8,128)(2,1)S(1)}, u32[]{:S(2)}, u32[]{:S(2)}) %collective-permute-start) | collective-permute-done | bytes 65568 | tf_op jit(solution)/shard_map/while/body/eval_jaxpr/ppermute | solution.py:19
  128.6 3.9 convolution_convert_fusion.1
  133.4 45.1 %reduce-scatter.3.cloned.1.call-done = bf16[16,4096]{1,0:T(8,128)(2,1)} async-done(((bf16[128,4096]{1,0:T(8,128)(2,1)}), bf16[16,4096]{1,0:T(8,128)(2,1)}) %reduce-scatter.3.cloned.1.call-update) | async-done | bytes 131088 | tf_op jit(solution)/shard_map/reduce_scatter | solution.py:123
  180.9 10.6 %all_to_all.10 = bf16[8,8,4096]{2,1,0:T(8,128)(2,1)} all-to-all(bf16[8,8,4096]{2,1,0:T(8,128)(2,1)S(1)} %fusion.24), channel_id=1, replica_groups=mesh['ctx'=16,'exp'=8] {'exp'}, dimensions={0} | all-to-all | bytes 1048576 | tf_op jit(solution)/shard_map/all_to_all | solution.py:131
  191.5 74.1 %all-gather.2.cloned.1.call-done = bf16[1024,4096]{1,0:T(8,128)(2,1)} async-done(((bf16[64,4096]{1,0:T(8,128)(2,1)}), bf16[1024,4096]{1,0:T(8,128)(2,1)}) %all-gather.2.cloned.1.call-update) | async-done | bytes 8388624 | tf_op jit(solution)/shard_map/all_gather | solution.py:137
  265.7 12.5 %fusion.20 = f32[1024,896]{1,0:T(8,128)S(1)} fusion(bf16[1024,4096]{1,0:T(8,128)(2,1)} %all-gather.2.cloned.1.call-done, bf16[1,4096,896]{2,1,0:T(8,128)(2,1)} %param.24), kind=kOutput, calls=%fused_computation.29 | convolution fusion | flops 7516192768 | bytes 19398656 | tf_op jit(solution)/shard_map/dot_general | solution.py:139
  278.2 12.0 %multiply_convert_fusion = bf16[1024,896]{1,0:T(8,128)(2,1)S(1)} fusion(f32[1024,896]{1,0:T(8,128)S(1)} %fusion.20, bf16[1024,4096]{1,0:T(8,128)(2,1)S(1)} %copy-done.5, bf16[1,4096,896]{2,1,0:T(8,128)(2,1)} %param.23), kind=kOutput, calls=%fused_computation.36 | convolution fusion | flops 7521697792 | bytes 21233664 | tf_op jit(solution)/shard_map/dot_general | solution.py:138
  290.2 11.1 %convolution_convert_fusion = bf16[1024,4096]{1,0:T(8,128)(2,1)} fusion(bf16[1024,896]{1,0:T(8,128)(2,1)S(1)} %multiply_convert_fusion, bf16[1,896,4096]{2,1,0:T(8,128)(2,1)S(1)} %bitcast.132), kind=kOutput, calls=%fused_computation.27 | convolution fusion | flops 7520387072 | bytes 17563648 | tf_op jit(solution)/shard_map/dot_general | solution.py:142
  301.3 99.6 %reduce-scatter.5.cloned.1.call-done = bf16[64,4096]{1,0:T(8,128)(2,1)} async-done(((bf16[1024,4096]{1,0:T(8,128)(2,1)}), bf16[64,4096]{1,0:T(8,128)(2,1)}) %reduce-scatter.5.cloned.1.call-update) | async-done | bytes 524304 | tf_op jit(solution)/shard_map/reduce_scatter | solution.py:141
  400.9 5.7 %all-to-all-start.1 = ((bf16[8,8,4096]{2,1,0:T(8,128)(2,1)}), bf16[8,8,4096]{2,1,0:T(8,128)(2,1)S(1)}, u32[]{:S(2)}, u32[]{:S(2)}) async-start(bf16[8,8,4096]{2,1,0:T(8,128)(2,1)} %bitcast.125), calls=%async_computation.3 | async-start | bytes 1048576 | tf_op jit(solution)/shard_map/all_to_all | solution.py:147
  407.0 6.7 %all-to-all-done.1 = bf16[8,8,4096]{2,1,0:T(8,128)(2,1)S(1)} async-done(((bf16[8,8,4096]{2,1,0:T(8,128)(2,1)}), bf16[8,8,4096]{2,1,0:T(8,128)(2,1)S(1)}, u32[]{:S(2)}, u32[]{:S(2)}) %all-to-all-start.1) | async-done | bytes 524320 | tf_op jit(solution)/shard_map/all_to_all | solution.py:147
  (232 shorter events, 42.7 us)
Async XLA Ops:
  6.5 172.0 %reduce-scatter.3.cloned.1.call-start = ((), (), s32[]{:S(2)}) async-start(), calls=%async_computation.4 | async-start | bytes 1179648 | tf_op jit(solution)/shard_map/reduce_scatter | solution.py:123
  10.8 121.8 %copy-start.3 = (s32[16,2]{0,1:T(2,128)S(1)}, s32[16,2]{0,1:T(2,128)}, u32[]{:S(2)}) copy-start(s32[16,2]{0,1:T(2,128)} %param.21) | copy-start | bytes 388
  10.8 167.7 %copy-start = (bf16[16,4096]{1,0:T(8,128)(2,1)S(1)}, bf16[16,4096]{1,0:T(8,128)(2,1)}, u32[]{:S(2)}) copy-start(bf16[16,4096]{1,0:T(8,128)(2,1)} %param.15) | copy-start | bytes 393220
  10.8 168.8 %copy-start.2 = (f32[4096]{0:T(1024)S(1)}, f32[4096]{0:T(1024)}, u32[]{:S(2)}) copy-start(f32[4096]{0:T(1024)} %param.20) | copy-start | bytes 49156
  10.9 3.5 collective-permute-start
  15.1 7.1 %collective-permute-start = (bf16[2,128,128]{2,1,0:T(8,128)(2,1)S(1)}, bf16[2,128,128]{2,1,0:T(8,128)(2,1)S(1)}, u32[]{:S(2)}, u32[]{:S(2)}) collective-permute-start(bf16[2,128,128]{2,1,0:T(8,128)(2,1)S(1)} %get-tuple-element.337), channel_id=1, source_target_pairs={{0,8},{8,16},{16,24},{24,32},{32,40},{40,48},{48,56},{56,64},{64,7... | collective-permute-start | bytes 196616 | tf_op jit(solution)/shard_map/while/body/eval_jaxpr/ppermute | solution.py:19
  22.9 7.1 %collective-permute-start = (bf16[2,128,128]{2,1,0:T(8,128)(2,1)S(1)}, bf16[2,128,128]{2,1,0:T(8,128)(2,1)S(1)}, u32[]{:S(2)}, u32[]{:S(2)}) collective-permute-start(bf16[2,128,128]{2,1,0:T(8,128)(2,1)S(1)} %get-tuple-element.337), channel_id=1, source_target_pairs={{0,8},{8,16},{16,24},{24,32},{32,40},{40,48},{48,56},{56,64},{64,7... | collective-permute-start | bytes 196616 | tf_op jit(solution)/shard_map/while/body/eval_jaxpr/ppermute | solution.py:19
  30.7 7.1 %collective-permute-start = (bf16[2,128,128]{2,1,0:T(8,128)(2,1)S(1)}, bf16[2,128,128]{2,1,0:T(8,128)(2,1)S(1)}, u32[]{:S(2)}, u32[]{:S(2)}) collective-permute-start(bf16[2,128,128]{2,1,0:T(8,128)(2,1)S(1)} %get-tuple-element.337), channel_id=1, source_target_pairs={{0,8},{8,16},{16,24},{24,32},{32,40},{40,48},{48,56},{56,64},{64,7... | collective-permute-start | bytes 196616 | tf_op jit(solution)/shard_map/while/body/eval_jaxpr/ppermute | solution.py:19
  38.6 7.1 %collective-permute-start = (bf16[2,128,128]{2,1,0:T(8,128)(2,1)S(1)}, bf16[2,128,128]{2,1,0:T(8,128)(2,1)S(1)}, u32[]{:S(2)}, u32[]{:S(2)}) collective-permute-start(bf16[2,128,128]{2,1,0:T(8,128)(2,1)S(1)} %get-tuple-element.337), channel_id=1, source_target_pairs={{0,8},{8,16},{16,24},{24,32},{32,40},{40,48},{48,56},{56,64},{64,7... | collective-permute-start | bytes 196616 | tf_op jit(solution)/shard_map/while/body/eval_jaxpr/ppermute | solution.py:19
  46.4 7.1 %collective-permute-start = (bf16[2,128,128]{2,1,0:T(8,128)(2,1)S(1)}, bf16[2,128,128]{2,1,0:T(8,128)(2,1)S(1)}, u32[]{:S(2)}, u32[]{:S(2)}) collective-permute-start(bf16[2,128,128]{2,1,0:T(8,128)(2,1)S(1)} %get-tuple-element.337), channel_id=1, source_target_pairs={{0,8},{8,16},{16,24},{24,32},{32,40},{40,48},{48,56},{56,64},{64,7... | collective-permute-start | bytes 196616 | tf_op jit(solution)/shard_map/while/body/eval_jaxpr/ppermute | solution.py:19
  54.2 7.1 %collective-permute-start = (bf16[2,128,128]{2,1,0:T(8,128)(2,1)S(1)}, bf16[2,128,128]{2,1,0:T(8,128)(2,1)S(1)}, u32[]{:S(2)}, u32[]{:S(2)}) collective-permute-start(bf16[2,128,128]{2,1,0:T(8,128)(2,1)S(1)} %get-tuple-element.337), channel_id=1, source_target_pairs={{0,8},{8,16},{16,24},{24,32},{32,40},{40,48},{48,56},{56,64},{64,7... | collective-permute-start | bytes 196616 | tf_op jit(solution)/shard_map/while/body/eval_jaxpr/ppermute | solution.py:19
  62.1 7.1 %collective-permute-start = (bf16[2,128,128]{2,1,0:T(8,128)(2,1)S(1)}, bf16[2,128,128]{2,1,0:T(8,128)(2,1)S(1)}, u32[]{:S(2)}, u32[]{:S(2)}) collective-permute-start(bf16[2,128,128]{2,1,0:T(8,128)(2,1)S(1)} %get-tuple-element.337), channel_id=1, source_target_pairs={{0,8},{8,16},{16,24},{24,32},{32,40},{40,48},{48,56},{56,64},{64,7... | collective-permute-start | bytes 196616 | tf_op jit(solution)/shard_map/while/body/eval_jaxpr/ppermute | solution.py:19
  69.9 7.1 %collective-permute-start = (bf16[2,128,128]{2,1,0:T(8,128)(2,1)S(1)}, bf16[2,128,128]{2,1,0:T(8,128)(2,1)S(1)}, u32[]{:S(2)}, u32[]{:S(2)}) collective-permute-start(bf16[2,128,128]{2,1,0:T(8,128)(2,1)S(1)} %get-tuple-element.337), channel_id=1, source_target_pairs={{0,8},{8,16},{16,24},{24,32},{32,40},{40,48},{48,56},{56,64},{64,7... | collective-permute-start | bytes 196616 | tf_op jit(solution)/shard_map/while/body/eval_jaxpr/ppermute | solution.py:19
  77.7 7.1 %collective-permute-start = (bf16[2,128,128]{2,1,0:T(8,128)(2,1)S(1)}, bf16[2,128,128]{2,1,0:T(8,128)(2,1)S(1)}, u32[]{:S(2)}, u32[]{:S(2)}) collective-permute-start(bf16[2,128,128]{2,1,0:T(8,128)(2,1)S(1)} %get-tuple-element.337), channel_id=1, source_target_pairs={{0,8},{8,16},{16,24},{24,32},{32,40},{40,48},{48,56},{56,64},{64,7... | collective-permute-start | bytes 196616 | tf_op jit(solution)/shard_map/while/body/eval_jaxpr/ppermute | solution.py:19
  85.5 7.2 %collective-permute-start = (bf16[2,128,128]{2,1,0:T(8,128)(2,1)S(1)}, bf16[2,128,128]{2,1,0:T(8,128)(2,1)S(1)}, u32[]{:S(2)}, u32[]{:S(2)}) collective-permute-start(bf16[2,128,128]{2,1,0:T(8,128)(2,1)S(1)} %get-tuple-element.337), channel_id=1, source_target_pairs={{0,8},{8,16},{16,24},{24,32},{32,40},{40,48},{48,56},{56,64},{64,7... | collective-permute-start | bytes 196616 | tf_op jit(solution)/shard_map/while/body/eval_jaxpr/ppermute | solution.py:19
  93.5 8.0 %collective-permute-start = (bf16[2,128,128]{2,1,0:T(8,128)(2,1)S(1)}, bf16[2,128,128]{2,1,0:T(8,128)(2,1)S(1)}, u32[]{:S(2)}, u32[]{:S(2)}) collective-permute-start(bf16[2,128,128]{2,1,0:T(8,128)(2,1)S(1)} %get-tuple-element.337), channel_id=1, source_target_pairs={{0,8},{8,16},{16,24},{24,32},{32,40},{40,48},{48,56},{56,64},{64,7... | collective-permute-start | bytes 196616 | tf_op jit(solution)/shard_map/while/body/eval_jaxpr/ppermute | solution.py:19
  102.3 8.0 %collective-permute-start = (bf16[2,128,128]{2,1,0:T(8,128)(2,1)S(1)}, bf16[2,128,128]{2,1,0:T(8,128)(2,1)S(1)}, u32[]{:S(2)}, u32[]{:S(2)}) collective-permute-start(bf16[2,128,128]{2,1,0:T(8,128)(2,1)S(1)} %get-tuple-element.337), channel_id=1, source_target_pairs={{0,8},{8,16},{16,24},{24,32},{32,40},{40,48},{48,56},{56,64},{64,7... | collective-permute-start | bytes 196616 | tf_op jit(solution)/shard_map/while/body/eval_jaxpr/ppermute | solution.py:19
  111.0 8.0 %collective-permute-start = (bf16[2,128,128]{2,1,0:T(8,128)(2,1)S(1)}, bf16[2,128,128]{2,1,0:T(8,128)(2,1)S(1)}, u32[]{:S(2)}, u32[]{:S(2)}) collective-permute-start(bf16[2,128,128]{2,1,0:T(8,128)(2,1)S(1)} %get-tuple-element.337), channel_id=1, source_target_pairs={{0,8},{8,16},{16,24},{24,32},{32,40},{40,48},{48,56},{56,64},{64,7... | collective-permute-start | bytes 196616 | tf_op jit(solution)/shard_map/while/body/eval_jaxpr/ppermute | solution.py:19
  119.7 8.0 %collective-permute-start = (bf16[2,128,128]{2,1,0:T(8,128)(2,1)S(1)}, bf16[2,128,128]{2,1,0:T(8,128)(2,1)S(1)}, u32[]{:S(2)}, u32[]{:S(2)}) collective-permute-start(bf16[2,128,128]{2,1,0:T(8,128)(2,1)S(1)} %get-tuple-element.337), channel_id=1, source_target_pairs={{0,8},{8,16},{16,24},{24,32},{32,40},{40,48},{48,56},{56,64},{64,7... | collective-permute-start | bytes 196616 | tf_op jit(solution)/shard_map/while/body/eval_jaxpr/ppermute | solution.py:19
  132.6 133.1 %all-gather.2.cloned.1.call-start = ((), (), s32[]{:S(2)}) async-start(), calls=%async_computation.5 | async-start | bytes 8912896 | tf_op jit(solution)/shard_map/all_gather | solution.py:137
  191.5 209.4 %reduce-scatter.5.cloned.1.call-start = ((), (), s32[]{:S(2)}) async-start(), calls=%async_computation.6 | async-start | bytes 8912896 | tf_op jit(solution)/shard_map/reduce_scatter | solution.py:141
  265.7 12.5 %copy-start.5 = (bf16[1024,4096]{1,0:T(8,128)(2,1)S(1)}, bf16[1024,4096]{1,0:T(8,128)(2,1)}, u32[]{:S(2)}) copy-start(bf16[1024,4096]{1,0:T(8,128)(2,1)} %all-gather.2.cloned.1.call-done) | copy-start | bytes 25165828
  265.7 24.5 %slice-start = ((s8[7340032]{0:T(1024)(128)(4,1)}), s8[4194304]{0:T(1024)(128)(4,1)S(1)}, s32[]{:S(2)}) async-start(s8[7340032]{0:T(1024)(128)(4,1)} %bitcast.131), calls=%async_computation.7 | async-start | bytes 8388608
  278.2 12.0 %slice-start.1 = ((s8[7340032]{0:T(1024)(128)(4,1)}), s8[3145728]{0:T(1024)(128)(4,1)S(1)}, s32[]{:S(2)}) async-start(s8[7340032]{0:T(1024)(128)(4,1)} %bitcast.131), calls=%async_computation.8 | async-start | bytes 6291456
  301.3 105.6 %copy-start.4 = (f32[16,2]{0,1:T(2,128)S(1)}, f32[16,2]{0,1:T(2,128)}, u32[]{:S(2)}) copy-start(f32[16,2]{0,1:T(2,128)} %param.22) | copy-start | bytes 388
  301.3 114.2 %copy-start.1 = (bf16[16,4096]{1,0:T(8,128)(2,1)S(1)}, bf16[16,4096]{1,0:T(8,128)(2,1)}, u32[]{:S(2)}) copy-start(bf16[16,4096]{1,0:T(8,128)(2,1)} %reduce-scatter.3.cloned.1.call-done) | copy-start | bytes 393220
  400.9 12.8 %all-to-all-start.1 = ((bf16[8,8,4096]{2,1,0:T(8,128)(2,1)}), bf16[8,8,4096]{2,1,0:T(8,128)(2,1)S(1)}, u32[]{:S(2)}, u32[]{:S(2)}) async-start(bf16[8,8,4096]{2,1,0:T(8,128)(2,1)} %bitcast.125), calls=%async_computation.3 | async-start | bytes 1048576 | tf_op jit(solution)/shard_map/all_to_all | solution.py:147
Sparse Core Ops, SparseCore 0:
  132.7 45.7 reduce-scatter.2
  191.6 74.0 all-gather.1
  301.5 99.4 reduce-scatter.4
where the time goes:
time: 428 us; the launch traced here: 423 us
  waiting for transfers between devices  312 us (73%)
  matrix products  50.1 us (12%)
  starting transfers between devices  25.3 us (6%)
  between operations  13.3 us (3%)
  blocking collectives  10.6 us (2%)
  other arithmetic  6.78 us (2%)
    reduce_scatter x1, waiting for transfers between devices, body(): lax.psum_scatter(jnp.dot(hidden_all, down_mat, preferred_element_type=jnp...  99.6 us
    ppermute x15, waiting for transfers between devices, passed_along(): return lax.ppermute(block, axis, route)  86.7 us
    all_gather x1, waiting for transfers between devices, body(): row_piece = lax.all_gather(rows_in, 'ctx', axis=0, tiled=True)  74.1 us
    reduce_scatter x1, waiting for transfers between devices, body(): lax.psum_scatter(jnp.dot(attention, out_weight, preferred_element_type=jn...  45.1 us
    ppermute x15, starting transfers between devices, passed_along(): return lax.ppermute(block, axis, route)  19.5 us
    dot_general x1, matrix products, body(): up_part = jnp.dot(row_piece, up_mat, preferred_element_type=jnp.float32)  12.5 us
    dot_general x1, matrix products, body(): gate_part = jnp.dot(row_piece, gate_mat, preferred_element_type=jnp.float32)  12 us
    dot_general x1, matrix products, body(): jnp.dot(hidden_all, down_mat, preferred_element_type=jnp.float32)  11.1 us
  transfers between devices with their start and end apart: 19, of which 19 were waited for; matrix products, arithmetic and copies ran while one was open for 0% of the time, Pallas kernels for 0%

commit v1 on v0

v1 whole, which is shorter than its diff:
```python
import functools
import math

import jax
import jax.numpy as jnp
from jax import lax
from jax.experimental import pallas as pl
from jax.experimental.pallas import tpu as pltpu
from jax.sharding import PartitionSpec as P

HD = 128
MESH = pl.DeviceIdType.MESH
NEG = -1e30
F32 = jnp.float32
BF = jnp.bfloat16
NT = (((1,), (1,)), ((), ()))
TN = (((0,), (0,)), ((), ()))


def layer_kernel(
    n_ctx,
    n_exp,
    q_ref,
    k_ref,
    v_ref,
    stream_ref,
    gain_ref,
    ids_ref,
    comb_ref,
    ow_hbm,
    wg_hbm,
    wu_hbm,
    wd_hbm,
    out_ref,
    k_all,
    v_all,
    m_s,
    l_s,
    acc_s,
    att_s,
    ow_v,
    wgu_v,
    wd_v,
    ps_v,
    pr_v,
    mixed_v,
    normed_v,
    pk_v,
    a2_v,
    rows_v,
    h_v,
    part_v,
    sib_v,
    rsb_v,
    ret_v,
    w_sem,
    kv_ss,
    kv_rs,
    ps_ss,
    ps_rs,
    a_ss,
    a_rs,
    ag_ss,
    ag_rs,
    fw_ss,
    fw_rs,
    sb_ss,
    sb_rs,
    ch_ss,
    ch_rs,
    r_ss,
    r_rs,
):
    c = lax.axis_index("ctx")
    e = lax.axis_index("exp")
    span = q_ref.shape[0]
    heads = q_ref.shape[1] // HD
    toks, dim = stream_ref.shape
    cap = pk_v.shape[1]
    slots = n_exp * cap
    n_chip = n_ctx // 2
    core = lax.rem(c, 2)
    chip = c // 2
    y = c // 4
    sibling = chip * 2 + 1 - core
    n_y = n_ctx // 4
    nt = wgu_v.shape[0]
    n_ps = ps_v.shape[0]
    ps_cols = ps_v.shape[3]

    def remote(src, dst, ss, rs, tc, te):
        return pltpu.make_async_remote_copy(
            src_ref=src, dst_ref=dst, send_sem=ss, recv_sem=rs, device_id=(tc, te), device_id_type=MESH
        )

    def weight_copies(n):
        cols = pl.ds(pl.multiple_of(n * HD, HD), HD)
        return (
            pltpu.make_async_copy(wg_hbm.at[:, cols], wgu_v.at[n, :, pl.ds(0, HD)], w_sem.at[0, n]),
            pltpu.make_async_copy(wu_hbm.at[:, cols], wgu_v.at[n, :, pl.ds(HD, HD)], w_sem.at[1, n]),
        )

    ow_copy = pltpu.make_async_copy(ow_hbm, ow_v, w_sem.at[2, 0])
    wd_copy = pltpu.make_async_copy(wd_hbm, wd_v, w_sem.at[2, 1])
    ow_copy.start()

    barrier = pltpu.get_barrier_semaphore()

    @pl.loop(1, n_ctx)
    def _(d):
        pl.semaphore_signal(barrier, inc=1, device_id=(lax.rem(c + d, n_ctx), e), device_id_type=MESH)

    @pl.loop(1, n_exp)
    def _(d):
        pl.semaphore_signal(barrier, inc=1, device_id=(c, lax.rem(e + d, n_exp)), device_id_type=MESH)

    pl.semaphore_wait(barrier, n_ctx - 1 + n_exp - 1)

    def kv_pair(j, src_block):
        return (
            remote(k_ref, k_all.at[src_block], kv_ss.at[0, j], kv_rs.at[0, src_block], j, e),
            remote(v_ref, v_all.at[src_block], kv_ss.at[1, j], kv_rs.at[1, src_block], j, e),
        )

    @pl.loop(c + 1, n_ctx)
    def _(j):
        for cp in kv_pair(j, c):
            cp.start()

    @pl.loop(0, nt)
    def _(n):
        for cp in weight_copies(n):
            cp.start()

    wd_copy.start()

    k_all[c] = k_ref[...]
    v_all[c] = v_ref[...]
    last_group = c // 4

    @pl.loop(c + 1, last_group * 4 + 4)
    def _(j):
        k_all[j] = jnp.zeros(k_ref.shape, BF)
        v_all[j] = jnp.zeros(v_ref.shape, BF)

    m_s[...] = jnp.full(m_s.shape, NEG, F32)
    l_s[...] = jnp.zeros(l_s.shape, F32)
    acc_s[...] = jnp.zeros(acc_s.shape, F32)
    scale = 1.0 / math.sqrt(HD)

    @pl.loop(0, last_group + 1)
    def _(g):
        @pl.loop(g * 4, jnp.minimum(g * 4 + 4, c))
        def _(j):
            for cp in kv_pair(c, j):
                cp.wait_recv()

        keys = k_all[pl.ds(g * 4, 4)].reshape(4 * span, HD)
        vals = v_all[pl.ds(g * 4, 4)].reshape(4 * span, HD)
        row = lax.broadcasted_iota(jnp.int32, (span, 4 * span), 0) + (c - g * 4) * span
        col = lax.broadcasted_iota(jnp.int32, (span, 4 * span), 1)
        allowed = row >= col
        for h in range(heads):
            s = lax.dot_general(q_ref[:, h * HD : (h + 1) * HD], keys, NT, preferred_element_type=F32) * scale
            s = jnp.where(allowed, s, NEG)
            m_old = m_s[h]
            m_new = jnp.maximum(m_old, jnp.max(s, axis=1, keepdims=True))
            p = jnp.exp(s - m_new[:, :1])
            fix = jnp.exp(m_old - m_new)
            l_s[h] = l_s[h] * fix + jnp.sum(p, axis=1, keepdims=True)
            acc_s[h] = acc_s[h] * fix + jnp.dot(p.astype(BF), vals, preferred_element_type=F32)
            m_s[h] = m_new

    for h in range(heads):
        att_s[:, h * HD : (h + 1) * HD] = (acc_s[h] / l_s[h]).astype(BF)

    ow_copy.wait()

    def ps_copy(n, te, src_e):
        return remote(ps_v.at[n, te], pr_v.at[n, src_e], ps_ss.at[n, te], ps_rs.at[n, src_e], c, te)

    @pl.loop(0, n_ps)
    def _(n):
        cols = pl.ds(pl.multiple_of(n * ps_cols, ps_cols), ps_cols)
        r = jnp.dot(att_s[...], ow_v[:, cols], preferred_element_type=F32)
        ps_v[n] = r.reshape(n_exp, toks, ps_cols).astype(BF)

        @pl.loop(1, n_exp)
        def _(d):
            ps_copy(n, lax.rem(e + d, n_exp), e).start()

        pr_v[n, e] = ps_v[n, e]

    @pl.loop(0, n_ps)
    def _(n):
        @pl.loop(1, n_exp)
        def _(d):
            ps_copy(n, e, lax.rem(e + d, n_exp)).wait_recv()

        cols = pl.ds(pl.multiple_of(n * ps_cols, ps_cols), ps_cols)
        total = jnp.sum(pr_v[n].astype(F32), axis=0)
        mixed_v[:, cols] = stream_ref[:, cols].astype(F32) + total

    mixed = mixed_v[...]
    mean_sq = jnp.mean(mixed * mixed, axis=1, keepdims=True)
    normed_v[...] = (mixed * lax.rsqrt(mean_sq + 1e-05) * gain_ref[...]).astype(BF)

    slot_row = lax.broadcasted_iota(jnp.int32, (slots, toks), 0)
    slot_exp = slot_row // cap
    first = ids_ref[0:1, :] == slot_exp
    second = ids_ref[1:2, :] == slot_exp
    named = jnp.where(first | second, 1.0, 0.0)
    tri = jnp.where(
        lax.broadcasted_iota(jnp.int32, (toks, toks), 0) < lax.broadcasted_iota(jnp.int32, (toks, toks), 1), 1.0, 0.0
    )
    rank = jnp.dot(named.astype(BF), tri.astype(BF), preferred_element_type=F32)
    slot_rank = (slot_row - slot_exp * cap).astype(F32)
    chosen = jnp.where(rank == slot_rank, named, 0.0)

    blk = 512

    @pl.loop(0, dim // blk)
    def _(j):
        cols = pl.ds(pl.multiple_of(j * blk, blk), blk)
        r = jnp.dot(chosen.astype(BF), normed_v[:, cols], preferred_element_type=F32)
        pk_v[:, :, cols] = r.reshape(n_exp, cap, blk).astype(BF)

    def a_copy(te, src_e):
        return remote(pk_v.at[te], a2_v.at[src_e], a_ss.at[te], a_rs.at[src_e], c, te)

    @pl.loop(1, n_exp)
    def _(d):
        a_copy(lax.rem(e + d, n_exp), e).start()

    a2_v[e] = pk_v[e]

    @pl.loop(1, n_exp)
    def _(d):
        a_copy(e, lax.rem(e + d, n_exp)).wait_recv()

    @pl.loop(0, dim // blk)
    def _(j):
        cols = pl.ds(pl.multiple_of(j * blk, blk), blk)
        rows_v[c, :, cols] = a2_v[:, :, cols].astype(F32).reshape(slots, blk).astype(BF)

    def ag_copy(to_chip, src_chip):
        b = src_chip * 2 + core
        return remote(rows_v.at[b], rows_v.at[b], ag_ss.at[to_chip], ag_rs.at[src_chip], to_chip * 2 + core, e)

    def fw_copy(src_chip, src_core):
        b = src_chip * 2 + src_core
        return remote(rows_v.at[b], rows_v.at[b], fw_ss.at[src_chip], fw_rs.at[src_chip], sibling, e)

    def step_off(s):
        return s ^ (s // 2)

    fw_copy(chip, core).start()

    xh = lax.rem(chip, 2)
    partner = chip + 1 - 2 * xh
    ag_copy(partner, chip).start()

    @pl.loop(1, n_y)
    def _(s):
        ty = lax.rem(y + n_y - step_off(s), n_y)
        ag_copy(ty * 2 + xh, chip).start()
        ag_copy(ty * 2 + 1 - xh, chip).start()

    ag_copy(chip, partner).wait_recv()
    fw_copy(partner, core).start()

    @pl.loop(0, nt)
    def _(n):
        for cp in weight_copies(n):
            cp.wait()

    wd_copy.wait()

    def sb_copy(q, of_core):
        return remote(part_v.at[q * 2 + of_core], sib_v.at[q], sb_ss.at[q], sb_rs.at[q], sibling, e)

    def ch_copy(to_chip, src_chip):
        return remote(
            part_v.at[to_chip * 2 + core],
            rsb_v.at[src_chip],
            ch_ss.at[to_chip],
            ch_rs.at[src_chip],
            to_chip * 2 + core,
            e,
        )

    def finish(yy):
        for x2 in range(2):
            q = yy * 2 + x2
            sb_copy(q, core).wait_recv()
            b = q * 2 + core

            @pl.loop(0, dim // blk)
            def _(j):
                cols = pl.ds(pl.multiple_of(j * blk, blk), blk)
                part_v[b, :, cols] = (part_v[b, :, cols].astype(F32) + sib_v[q, :, cols].astype(F32)).astype(BF)

            @pl.when(q != chip)
            def _():
                ch_copy(q, chip).start()

    rows_chunk = 4 * slots

    @pl.loop(0, n_y)
    def _(s):
        yy = lax.rem(y + step_off(s), n_y)
        for x2 in range(2):
            fw_copy(yy * 2 + x2, 1 - core).wait_recv()

        @pl.loop(0, nt)
        def _(n):
            x = rows_v[pl.ds(yy * 4, 4)].reshape(rows_chunk, dim)
            r = jnp.dot(x, wgu_v[n], preferred_element_type=F32)
            g = r[:, :HD]
            u = r[:, HD:]
            h_v[:, pl.ds(pl.multiple_of(n * HD, HD), HD)] = (g / (1.0 + jnp.exp(-g)) * u).astype(BF)

        @pl.when(s < n_y - 1)
        def _():
            y2 = lax.rem(y + step_off(s + 1), n_y)
            for x2 in range(2):
                q = y2 * 2 + x2
                ag_copy(chip, q).wait_recv()
                fw_copy(q, core).start()

        @pl.when(s > 0)
        def _():
            finish(lax.rem(y + step_off(s - 1), n_y))

        @pl.loop(0, dim // blk)
        def _(j):
            cols = pl.ds(pl.multiple_of(j * blk, blk), blk)
            o = jnp.dot(h_v[...], wd_v[:, cols], preferred_element_type=F32)
            part_v[pl.ds(yy * 4, 4), :, cols] = o.astype(BF).reshape(4, slots, blk)

        for x2 in range(2):
            sb_copy(yy * 2 + x2, 1 - core).start()

    finish(lax.rem(y + step_off(n_y - 1), n_y))

    @pl.loop(1, n_chip)
    def _(d):
        ch_copy(chip, lax.rem(chip + d, n_chip)).wait_recv()

    @pl.loop(1, n_exp)
    def _(d):
        a_copy(lax.rem(e + d, n_exp), e).wait_send()

    @pl.loop(0, dim // blk)
    def _(j):
        cols = pl.ds(pl.multiple_of(j * blk, blk), blk)
        rsb_v[chip, :, cols] = part_v[c, :, cols]
        r = jnp.sum(rsb_v[:, :, cols].astype(F32), axis=0)
        pk_v[:, :, cols] = r.reshape(n_exp, cap, blk).astype(BF)

    def r_copy(te, src_e):
        return remote(pk_v.at[te], ret_v.at[src_e], r_ss.at[te], r_rs.at[src_e], c, te)

    @pl.loop(1, n_exp)
    def _(d):
        r_copy(lax.rem(e + d, n_exp), e).start()

    ret_v[e] = pk_v[e]

    wt = chosen * jnp.where(first, comb_ref[0:1, :], comb_ref[1:2, :])
    w_hi = wt.astype(BF)
    w_lo = (wt - w_hi.astype(F32)).astype(BF)

    @pl.loop(1, n_exp)
    def _(d):
        r_copy(e, lax.rem(e + d, n_exp)).wait_recv()

    @pl.loop(0, dim // blk)
    def _(j):
        cols = pl.ds(pl.multiple_of(j * blk, blk), blk)
        r = ret_v[:, :, cols].astype(F32).reshape(slots, blk).astype(BF)
        o = lax.dot_general(w_hi, r, TN, preferred_element_type=F32)
        o = o + lax.dot_general(w_lo, r, TN, preferred_element_type=F32)
        out_ref[:, cols] = (mixed_v[:, cols] + o).astype(BF)

    @pl.loop(c + 1, n_ctx)
    def _(j):
        for cp in kv_pair(j, c):
            cp.wait_send()

    @pl.loop(1, n_exp)
    def _(d):
        te = lax.rem(e + d, n_exp)

        @pl.loop(0, n_ps)
        def _(n):
            ps_copy(n, te, e).wait_send()

        r_copy(te, e).wait_send()

    @pl.loop(1, n_chip)
    def _(d):
        q = lax.rem(chip + d, n_chip)
        ag_copy(q, chip).wait_send()
        ch_copy(q, chip).wait_send()

    @pl.loop(0, n_chip)
    def _(q):
        fw_copy(q, core).wait_send()
        sb_copy(q, 1 - core).wait_send()


def body(
    stream, queries, attn_keys, attn_values, out_weight, norm_gain, expert_ids, combine, w_gate, w_up, w_down
):
    n_ctx = lax.axis_size("ctx")
    n_exp = lax.axis_size("exp")
    span, qw = queries.shape
    toks, dim = stream.shape
    hid = w_gate.shape[2]
    heads = qw // HD
    cap = toks // 2
    slots = n_exp * cap
    n_chip = n_ctx // 2
    nt = hid // HD
    n_ps = 4
    vm = pl.BlockSpec(memory_space=pltpu.VMEM)
    hbm = pl.BlockSpec(memory_space=pl.ANY)
    dma = pltpu.SemaphoreType.DMA
    scratch = [
        pltpu.VMEM((n_ctx, span, HD), BF),
        pltpu.VMEM((n_ctx, span, HD), BF),
        pltpu.VMEM((heads, span, HD), F32),
        pltpu.VMEM((heads, span, HD), F32),
        pltpu.VMEM((heads, span, HD), F32),
        pltpu.VMEM((span, qw), BF),
        pltpu.VMEM((qw, dim), BF),
        pltpu.VMEM((nt, dim, 2 * HD), BF),
        pltpu.VMEM((hid, dim), BF),
        pltpu.VMEM((n_ps, n_exp, toks, dim // n_ps), BF),
        pltpu.VMEM((n_ps, n_exp, toks, dim // n_ps), BF),
        pltpu.VMEM((toks, dim), F32),
        pltpu.VMEM((toks, dim), BF),
        pltpu.VMEM((n_exp, cap, dim), BF),
        pltpu.VMEM((n_exp, cap, dim), BF),
        pltpu.VMEM((n_ctx, slots, dim), BF),
        pltpu.VMEM((4 * slots, hid), BF),
        pltpu.VMEM((n_ctx, slots, dim), BF),
        pltpu.VMEM((n_chip, slots, dim), BF),
        pltpu.VMEM((n_chip, slots, dim), BF),
        pltpu.VMEM((n_exp, cap, dim), BF),
        dma((3, nt)),
        dma((2, n_ctx)),
        dma((2, n_ctx)),
        dma((n_ps, n_exp)),
        dma((n_ps, n_exp)),
        dma((n_exp,)),
        dma((n_exp,)),
        dma((n_chip,)),
        dma((n_chip,)),
        dma((n_chip,)),
        dma((n_chip,)),
        dma((n_chip,)),
        dma((n_chip,)),
        dma((n_chip,)),
        dma((n_chip,)),
        dma((n_exp,)),
        dma((n_exp,)),
    ]
    return pl.pallas_call(
        functools.partial(layer_kernel, n_ctx, n_exp),
        out_shape=jax.ShapeDtypeStruct((toks, dim), BF),
        in_specs=[vm] * 7 + [hbm] * 4,
        out_specs=vm,
        scratch_shapes=scratch,
        compiler_params=pltpu.CompilerParams(
            collective_id=0, has_side_effects=True, vmem_limit_bytes=67_000_000
        ),
        name="decoder_layer",
    )(
        queries,
        attn_keys,
        attn_values,
        stream,
        norm_gain.reshape(1, dim),
        expert_ids.T,
        combine.T,
        out_weight,
        w_gate[0],
        w_up[0],
        w_down[0],
    )


def solution(mesh):
    in_specs = (
        P(("ctx", "exp"), None),
        P("ctx", "exp"),
        P("ctx", "exp"),
        P("ctx", "exp"),
        P("exp", None),
        P(),
        P(("ctx", "exp"), None),
        P(("ctx", "exp"), None),
        P("exp", None, "ctx"),
        P("exp", None, "ctx"),
        P("exp", "ctx", None),
    )
    out_specs = P(("ctx", "exp"), None)
    return jax.shard_map(body, mesh=mesh, in_specs=in_specs, out_specs=out_specs, check_vma=False)
```

time: 428 us -> 176 us (0.41); the launches traced: 423 us -> 176 us
  waiting for transfers between devices: 312 us -> 0 us
  Pallas kernels: 0 us -> 174 us
  matrix products: 50.1 us -> 0 us
  starting transfers between devices: 25.3 us -> 0 us
  between operations: 13.3 us -> 0.01 us
  blocking collectives: 10.6 us -> 0 us
  other arithmetic: 6.78 us -> 0 us
    pallas_call x0 -> x1, Pallas kernels: none -> 174 us  [body(): pl.pallas_call(functools.partial(layer_kernel, n_ctx, n_exp), out_shape=j...]
    reduce_scatter x2 -> x0, waiting for transfers between devices: 145 us -> none  [the longest x1 99.6 us: body(): lax.psum_scatter(jnp.dot(hidden_all, down_mat, preferred_element_type=jnp...]
    ppermute x15 -> x0, waiting for transfers between devices: 86.7 us -> none  [passed_along(): return lax.ppermute(block, axis, route)]
    all_gather x1 -> x0, waiting for transfers between devices: 74.1 us -> none  [body(): row_piece = lax.all_gather(rows_in, 'ctx', axis=0, tiled=True)]
    dot_general x37 -> x0, matrix products: 50.1 us -> none  [the longest x1 12.5 us: body(): up_part = jnp.dot(row_piece, up_mat, preferred_element_type=jnp.float32)]
    ppermute x15 -> x0, starting transfers between devices: 19.5 us -> none  [passed_along(): return lax.ppermute(block, axis, route)]
    all_to_all x1 -> x0, blocking collectives: 10.6 us -> none  [body(): lax.all_to_all(outgoing.reshape(n_exp, capacity, model_dim), 'exp', split...]
    all_to_all x1 -> x0, waiting for transfers between devices: 6.75 us -> none  [body(): lax.all_to_all(expert_result.reshape(n_exp, capacity, model_dim), 'exp',...]
  transfers between devices with their start and end apart: 19 -> 0, of which waited for: 19 -> 0; matrix products, arithmetic and copies ran while one was open for 0% -> 0% of each run, Pallas kernels for 0% -> 0%
where the time goes in v1:
time: 176 us
  Pallas kernels  174 us (99%)
    pallas_call x1, Pallas kernels, body(): pl.pallas_call(functools.partial(layer_kernel, n_ctx, n_exp), out_shape=j...  174 us

profile of v1, /device:TPU:29, one launch (start us, length us, event | category | flops | bytes accessed | tf_op | source)
XLA Modules:
  0.0 175.9 jit_solution(8544688298184107239)
XLA Ops:
  0.0 174.3 %decoder_layer.1 = bf16[16,4096]{1,0:T(8,128)(2,1)} custom-call(bf16[128,512]{1,0:T(8,128)(2,1)} %q_ref.1, bf16[128,128]{1,0:T(8,128)(2,1)} %k_ref.1, bf16[128,128]{1,0:T(8,128)(2,1)} %v_ref.1, bf16[16,4096]{1,0:T(8,128)(2,1)} %stream_ref.1, f32[1,4096]{1,0:T(1,128)} %bitcast.9, s32[2,16]{1,0:T(2,128)} %bitcast.10, f32[2,16]{1,0:T(2,128)} %bitcast.11, ...), custom_call_target="tpu_custom_call" | custom-call | tf_op jit(solution)/shard_map/decoder_layer/pallas_call | solution.py:470
  174.3 1.6 copy.13

commit v2 on v1

v2 whole, which is shorter than its diff:
```python
import functools
import math

import jax
import jax.numpy as jnp
from jax import lax
from jax.experimental import pallas as pl
from jax.experimental.pallas import tpu as pltpu
from jax.sharding import PartitionSpec as P

HD = 128
MESH = pl.DeviceIdType.MESH
NEG = -1e30
F32 = jnp.float32
BF = jnp.bfloat16
NT = (((1,), (1,)), ((), ()))
TN = (((0,), (0,)), ((), ()))


def layer_kernel(
    n_ctx,
    n_exp,
    q_ref,
    k_ref,
    v_ref,
    stream_ref,
    gain_ref,
    ids_ref,
    comb_ref,
    ow_hbm,
    wg_hbm,
    wu_hbm,
    wd_hbm,
    out_ref,
    k_all,
    v_all,
    m_s,
    l_s,
    acc_s,
    att_s,
    ow_v,
    wgu_v,
    wd_v,
    ps_v,
    pr_v,
    mixed_v,
    normed_v,
    pk_v,
    a2_v,
    rows_v,
    h_v,
    part_v,
    sib_v,
    rh0_v,
    rx1_v,
    rh1_v,
    rx0_v,
    ret_v,
    w_sem,
    kv_ss,
    kv_rs,
    kf_ss,
    ps_ss,
    ps_rs,
    a_ss,
    a_rs,
    ag_ss,
    ag_rs,
    rl_ss,
    fw_ss,
    fw_rs,
    sb_ss,
    sb_rs,
    c0_ss,
    c0_rs,
    x1_ss,
    x1_rs,
    c1_ss,
    c1_rs,
    x0_ss,
    x0_rs,
    r_ss,
    r_rs,
):
    c = lax.axis_index("ctx")
    e = lax.axis_index("exp")
    span = q_ref.shape[0]
    heads = q_ref.shape[1] // HD
    toks, dim = stream_ref.shape
    cap = pk_v.shape[1]
    slots = n_exp * cap
    n_chip = n_ctx // 2
    core = lax.rem(c, 2)
    chip = c // 2
    y = c // 4
    xh = lax.rem(chip, 2)
    partner = chip + 1 - 2 * xh
    sibling = chip * 2 + 1 - core
    n_y = n_ctx // 4
    nt = wgu_v.shape[0]
    n_ps = ps_v.shape[0]
    ps_cols = ps_v.shape[3]
    blk = 512
    w0 = rh0_v.shape[3]
    w1 = dim - w0
    begin = (w1, 0)
    width = (w0, w1)

    def piece(h):
        return pl.ds(begin[h], width[h])

    def each_block(h, do):
        @pl.loop(0, width[h] // blk)
        def _(j):
            near = pl.multiple_of(j * blk, blk)
            do(pl.ds(pl.multiple_of(begin[h] + near, blk), blk), pl.ds(near, blk))

    def remote(src, dst, ss, rs, tc, te):
        return pltpu.make_async_remote_copy(
            src_ref=src, dst_ref=dst, send_sem=ss, recv_sem=rs, device_id=(tc, te), device_id_type=MESH
        )

    def weight_copies(n):
        cols = pl.ds(pl.multiple_of(n * HD, HD), HD)
        return (
            pltpu.make_async_copy(wg_hbm.at[:, cols], wgu_v.at[n, :, pl.ds(0, HD)], w_sem.at[0, n]),
            pltpu.make_async_copy(wu_hbm.at[:, cols], wgu_v.at[n, :, pl.ds(HD, HD)], w_sem.at[1, n]),
        )

    ow_copy = pltpu.make_async_copy(ow_hbm, ow_v, w_sem.at[2, 0])
    wd_copy = pltpu.make_async_copy(wd_hbm, wd_v, w_sem.at[2, 1])
    ow_copy.start()

    barrier = pltpu.get_barrier_semaphore()
    pl.semaphore_signal(barrier, inc=1, device_id=(sibling, e), device_id_type=MESH)

    @pl.loop(1, n_chip)
    def _(d):
        tc = lax.rem(chip + d, n_chip) * 2 + core
        pl.semaphore_signal(barrier, inc=1, device_id=(tc, e), device_id_type=MESH)

    @pl.loop(1, n_exp)
    def _(d):
        pl.semaphore_signal(barrier, inc=1, device_id=(c, lax.rem(e + d, n_exp)), device_id_type=MESH)

    pl.semaphore_wait(barrier, n_chip + n_exp - 1)

    def kv_pair(to_chip, block):
        return (
            remote(k_ref, k_all.at[block], kv_ss.at[0, to_chip], kv_rs.at[0, block], to_chip * 2 + core, e),
            remote(v_ref, v_all.at[block], kv_ss.at[1, to_chip], kv_rs.at[1, block], to_chip * 2 + core, e),
        )

    def kv_own():
        return (
            remote(k_ref, k_all.at[c], kf_ss.at[0, chip], kv_rs.at[0, c], sibling, e),
            remote(v_ref, v_all.at[c], kf_ss.at[1, chip], kv_rs.at[1, c], sibling, e),
        )

    def kv_forward(q):
        b = q * 2 + core
        return (
            remote(k_all.at[b], k_all.at[b], kf_ss.at[0, q], kv_rs.at[0, b], sibling, e),
            remote(v_all.at[b], v_all.at[b], kf_ss.at[1, q], kv_rs.at[1, b], sibling, e),
        )

    @pl.when(core == 0)
    def _():
        for cp in kv_own():
            cp.start()

    @pl.loop(chip + 1, n_chip)
    def _(q):
        for cp in kv_pair(q, c):
            cp.start()

    @pl.loop(0, nt)
    def _(n):
        for cp in weight_copies(n):
            cp.start()

    wd_copy.start()

    k_all[c] = k_ref[...]
    v_all[c] = v_ref[...]

    @pl.loop(c + 1, y * 4 + 4)
    def _(j):
        k_all[j] = jnp.zeros(k_ref.shape, BF)
        v_all[j] = jnp.zeros(v_ref.shape, BF)

    m_s[...] = jnp.full(m_s.shape, NEG, F32)
    l_s[...] = jnp.zeros(l_s.shape, F32)
    acc_s[...] = jnp.zeros(acc_s.shape, F32)
    scale = 1.0 / math.sqrt(HD)

    def step_off(s):
        return s ^ (s // 2)

    def forward_group(g):
        @pl.loop(g * 2, jnp.minimum(g * 2 + 2, chip))
        def _(q):
            for cp in kv_pair(chip, q * 2 + core):
                cp.wait_recv()
            for cp in kv_forward(q):
                cp.start()

    forward_group(y)

    @pl.loop(0, n_y)
    def _(s):
        g = y - step_off(s)
        g2 = y - step_off(s + 1)

        @pl.when((s < n_y - 1) & (g2 >= 0))
        def _():
            forward_group(g2)

        @pl.when(g >= 0)
        def _():
            @pl.loop(g * 2, jnp.minimum(g * 2 + 2, (c + core) // 2))
            def _(q):
                for cp in kv_pair(chip, q * 2 + 1 - core):
                    cp.wait_recv()

            keys = k_all[pl.ds(g * 4, 4)].reshape(4 * span, HD)
            vals = v_all[pl.ds(g * 4, 4)].reshape(4 * span, HD)
            row = lax.broadcasted_iota(jnp.int32, (span, 4 * span), 0) + (c - g * 4) * span
            col = lax.broadcasted_iota(jnp.int32, (span, 4 * span), 1)
            allowed = row >= col
            for h in range(heads):
                q_h = q_ref[:, h * HD : (h + 1) * HD]
                s_h = lax.dot_general(q_h, keys, NT, preferred_element_type=F32) * scale
                s_h = jnp.where(allowed, s_h, NEG)
                m_old = m_s[h]
                m_new = jnp.maximum(m_old, jnp.max(s_h, axis=1, keepdims=True))
                p = jnp.exp(s_h - m_new[:, :1])
                fix = jnp.exp(m_old - m_new)
                l_s[h] = l_s[h] * fix + jnp.sum(p, axis=1, keepdims=True)
                acc_s[h] = acc_s[h] * fix + jnp.dot(p.astype(BF), vals, preferred_element_type=F32)
                m_s[h] = m_new

    for h in range(heads):
        att_s[:, h * HD : (h + 1) * HD] = (acc_s[h] / l_s[h]).astype(BF)

    ow_copy.wait()

    def ps_copy(n, te, src_e):
        return remote(ps_v.at[n, te], pr_v.at[n, src_e], ps_ss.at[n, te], ps_rs.at[n, src_e], c, te)

    @pl.loop(0, n_ps)
    def _(n):
        cols = pl.ds(pl.multiple_of(n * ps_cols, ps_cols), ps_cols)
        r = jnp.dot(att_s[...], ow_v[:, cols], preferred_element_type=F32)
        ps_v[n] = r.reshape(n_exp, toks, ps_cols).astype(BF)

        @pl.loop(1, n_exp)
        def _(d):
            ps_copy(n, lax.rem(e + d, n_exp), e).start()

        pr_v[n, e] = ps_v[n, e]

    slot_row = lax.broadcasted_iota(jnp.int32, (slots, toks), 0)
    slot_exp = slot_row // cap
    first = ids_ref[0:1, :] == slot_exp
    second = ids_ref[1:2, :] == slot_exp
    named = jnp.where(first | second, 1.0, 0.0)
    tri = jnp.where(
        lax.broadcasted_iota(jnp.int32, (toks, toks), 0) < lax.broadcasted_iota(jnp.int32, (toks, toks), 1), 1.0, 0.0
    )
    rank = jnp.dot(named.astype(BF), tri.astype(BF), preferred_element_type=F32)
    slot_rank = (slot_row - slot_exp * cap).astype(F32)
    chosen = jnp.where(rank == slot_rank, named, 0.0)
    chosen_bf = chosen.astype(BF)

    @pl.loop(0, n_ps)
    def _(n):
        @pl.loop(1, n_exp)
        def _(d):
            ps_copy(n, e, lax.rem(e + d, n_exp)).wait_recv()

        cols = pl.ds(pl.multiple_of(n * ps_cols, ps_cols), ps_cols)
        total = jnp.sum(pr_v[n].astype(F32), axis=0)
        mixed_v[:, cols] = stream_ref[:, cols].astype(F32) + total

    mixed = mixed_v[...]
    mean_sq = jnp.mean(mixed * mixed, axis=1, keepdims=True)
    normed_v[...] = (mixed * lax.rsqrt(mean_sq + 1e-05) * gain_ref[...]).astype(BF)

    def a_copy(te, src_e, h):
        return remote(
            pk_v.at[te, :, piece(h)], a2_v.at[src_e, :, piece(h)], a_ss.at[h, te], a_rs.at[h, src_e], c, te
        )

    for h in (0, 1):

        def pick(cols, near):
            r = jnp.dot(chosen_bf, normed_v[:, cols], preferred_element_type=F32)
            pk_v[:, :, cols] = r.reshape(n_exp, cap, blk).astype(BF)

        each_block(h, pick)

        @pl.loop(1, n_exp)
        def _(d):
            a_copy(lax.rem(e + d, n_exp), e, h).start()

    a2_v[e] = pk_v[e]

    def row_copy(to_chip, q, h, ss):
        part = rows_v.at[q * 2 + core, :, piece(h)]
        return remote(part, part, ss, ag_rs.at[h, q], to_chip * 2 + core, e)

    def own_copy(to_chip, h):
        return row_copy(to_chip, chip, h, ag_ss.at[h, to_chip])

    def arrived(q, h):
        row_copy(chip, q, h, ag_ss.at[h, chip]).wait_recv()

    def relay_y(ty):
        return row_copy(ty * 2 + xh, partner, 0, rl_ss.at[0, ty])

    def relay_x(yy):
        return row_copy(partner, yy * 2 + xh, 1, rl_ss.at[1, yy])

    def fw_copy(q, of_core, h):
        part = rows_v.at[q * 2 + of_core, :, piece(h)]
        return remote(part, part, fw_ss.at[h, q], fw_rs.at[h, q], sibling, e)

    def down_y(s):
        return lax.rem(y + n_y - step_off(s), n_y)

    def up_y(s):
        return lax.rem(y + step_off(s), n_y)

    for h in (0, 1):

        @pl.loop(1, n_exp)
        def _(d):
            a_copy(e, lax.rem(e + d, n_exp), h).wait_recv()

        def settle(cols, near):
            rows_v[c, :, cols] = a2_v[:, :, cols].astype(F32).reshape(slots, blk).astype(BF)

        each_block(h, settle)
        own_copy(partner, h).start()

        @pl.loop(1, n_y)
        def _(s):
            own_copy(down_y(s) * 2 + xh, h).start()

        fw_copy(chip, core, h).start()

    def column_rows(s):
        q = up_y(s) * 2 + xh
        arrived(q, 0)
        fw_copy(q, core, 0).start()
        arrived(q, 1)
        relay_x(up_y(s)).start()
        fw_copy(q, core, 1).start()

    def other_rows(s):
        q = up_y(s) * 2 + 1 - xh
        for h in (0, 1):
            arrived(q, h)
            fw_copy(q, core, h).start()

    arrived(partner, 0)

    @pl.loop(1, n_y)
    def _(s):
        relay_y(down_y(s)).start()

    fw_copy(partner, core, 0).start()
    arrived(partner, 1)
    fw_copy(partner, core, 1).start()

    @pl.loop(1, n_y - 1)
    def _(s):
        column_rows(s)

    @pl.loop(0, nt)
    def _(n):
        for cp in weight_copies(n):
            cp.wait()

    wd_copy.wait()

    def sb_copy(q, of_core, h):
        return remote(
            part_v.at[q * 2 + of_core, :, piece(h)],
            sib_v.at[q, :, piece(h)],
            sb_ss.at[h, q],
            sb_rs.at[h, q],
            sibling,
            e,
        )

    def c0_copy(yy, x2, src_y):
        return remote(
            part_v.at[(yy * 2 + x2) * 2 + core, :, piece(0)],
            rh0_v.at[src_y, x2],
            c0_ss.at[yy, x2],
            c0_rs.at[src_y, x2],
            (yy * 2 + xh) * 2 + core,
            e,
        )

    def x1_copy(yy):
        return remote(
            part_v.at[(yy * 2 + 1 - xh) * 2 + core, :, piece(1)],
            rx1_v.at[yy],
            x1_ss.at[yy],
            x1_rs.at[yy],
            partner * 2 + core,
            e,
        )

    def c1_copy(yy, src_y):
        b = (yy * 2 + xh) * 2 + core
        return remote(part_v.at[b, :, piece(1)], rh1_v.at[src_y], c1_ss.at[yy], c1_rs.at[src_y], b, e)

    def x0_copy():
        return remote(
            part_v.at[partner * 2 + core, :, piece(0)], rx0_v, x0_ss.at[0], x0_rs.at[0], partner * 2 + core, e
        )

    def over_cores(yy):
        for h in (1, 0):
            for x2 in range(2):
                q = yy * 2 + x2
                b = q * 2 + core
                sb_copy(q, core, h).wait_recv()

                def add(cols, near):
                    total = part_v[b, :, cols].astype(F32) + sib_v[q, :, cols].astype(F32)
                    part_v[b, :, cols] = total.astype(BF)

                each_block(h, add)
            if h == 1:
                x1_copy(yy).start()
            else:

                @pl.when(yy != y)
                def _():
                    for x2 in range(2):
                        c0_copy(yy, x2, y).start()

    def over_x(yy):
        x1_copy(yy).wait_recv()
        b = (yy * 2 + xh) * 2 + core

        def add(cols, near):
            total = part_v[b, :, cols].astype(F32) + rx1_v[yy, :, near].astype(F32)
            part_v[b, :, cols] = total.astype(BF)

        each_block(1, add)

        @pl.when(yy != y)
        def _():
            c1_copy(yy, y).start()

    rows_chunk = 4 * slots
    dn = 1024

    @pl.loop(0, n_y)
    def _(s):
        yy = up_y(s)

        @pl.when(s == 1)
        def _():
            other_rows(1)

        for x2 in range(2):
            for h in (0, 1):
                fw_copy(yy * 2 + x2, 1 - core, h).wait_recv()

        @pl.loop(0, nt)
        def _(n):
            x = rows_v[pl.ds(yy * 4, 4)].reshape(rows_chunk, dim)
            r = jnp.dot(x, wgu_v[n], preferred_element_type=F32)
            g = r[:, :HD]
            u = r[:, HD:]
            h_v[:, pl.ds(pl.multiple_of(n * HD, HD), HD)] = (g / (1.0 + jnp.exp(-g)) * u).astype(BF)

        @pl.when(s == 0)
        def _():
            column_rows(n_y - 1)

        @pl.when((s > 0) & (s < n_y - 1))
        def _():
            other_rows(s + 1)

        @pl.when(s > 0)
        def _():
            over_cores(up_y(s - 1))

        @pl.when(s > 1)
        def _():
            over_x(up_y(s - 2))

        def down(j):
            cols = pl.ds(pl.multiple_of(j * dn, dn), dn)
            o = jnp.dot(h_v[...], wd_v[:, cols], preferred_element_type=F32)
            part_v[pl.ds(yy * 4, 4), :, cols] = o.astype(BF).reshape(4, slots, dn)

        early = -(-w1 // dn)
        pl.loop(0, early)(down)
        for x2 in range(2):
            sb_copy(yy * 2 + x2, 1 - core, 1).start()
        pl.loop(early, dim // dn)(down)
        for x2 in range(2):
            sb_copy(yy * 2 + x2, 1 - core, 0).start()

    over_cores(up_y(n_y - 1))
    over_x(up_y(n_y - 2))
    over_x(up_y(n_y - 1))

    @pl.loop(1, n_y)
    def _(d):
        for x2 in range(2):
            c0_copy(y, x2, lax.rem(y + d, n_y)).wait_recv()

    def column_sum(b, x2, cols, near):
        total = part_v[b, :, cols].astype(F32)
        for d in range(1, n_y):
            total = total + rh0_v[lax.rem(y + d, n_y), x2, :, near].astype(F32)
        return total

    def to_partner(cols, near):
        b = partner * 2 + core
        part_v[b, :, cols] = column_sum(b, 1 - xh, cols, near).astype(BF)

    each_block(0, to_partner)
    x0_copy().start()

    def r_copy(te, src_e, h):
        return remote(
            pk_v.at[te, :, piece(h)], ret_v.at[src_e, :, piece(h)], r_ss.at[h, te], r_rs.at[h, src_e], c, te
        )

    @pl.loop(1, n_exp)
    def _(d):
        for h in (0, 1):
            a_copy(lax.rem(e + d, n_exp), e, h).wait_send()

    def give_back(cols, total):
        pk_v[:, :, cols] = total.reshape(n_exp, cap, blk).astype(BF)

    for h in (1, 0):
        if h == 1:

            @pl.loop(1, n_y)
            def _(d):
                c1_copy(y, lax.rem(y + d, n_y)).wait_recv()

            def whole(cols, near):
                total = part_v[c, :, cols].astype(F32)
                for d in range(1, n_y):
                    total = total + rh1_v[lax.rem(y + d, n_y), :, near].astype(F32)
                give_back(cols, total)

        else:
            x0_copy().wait_recv()

            def whole(cols, near):
                give_back(cols, column_sum(c, xh, cols, near) + rx0_v[:, near].astype(F32))

        each_block(h, whole)

        @pl.loop(1, n_exp)
        def _(d):
            r_copy(lax.rem(e + d, n_exp), e, h).start()

    ret_v[e] = pk_v[e]

    wt = chosen * jnp.where(first, comb_ref[0:1, :], comb_ref[1:2, :])
    w_hi = wt.astype(BF)
    w_lo = (wt - w_hi.astype(F32)).astype(BF)

    for h in (1, 0):

        @pl.loop(1, n_exp)
        def _(d):
            r_copy(e, lax.rem(e + d, n_exp), h).wait_recv()

        def combine(cols, near):
            r = ret_v[:, :, cols].astype(F32).reshape(slots, blk).astype(BF)
            o = lax.dot_general(w_hi, r, TN, preferred_element_type=F32)
            o = o + lax.dot_general(w_lo, r, TN, preferred_element_type=F32)
            out_ref[:, cols] = (mixed_v[:, cols] + o).astype(BF)

        each_block(h, combine)

    @pl.when(core == 0)
    def _():
        for cp in kv_own():
            cp.wait_send()

    @pl.loop(chip + 1, n_chip)
    def _(q):
        for cp in kv_pair(q, c):
            cp.wait_send()

    @pl.loop(0, chip)
    def _(q):
        for cp in kv_forward(q):
            cp.wait_send()

    @pl.loop(1, n_exp)
    def _(d):
        te = lax.rem(e + d, n_exp)

        @pl.loop(0, n_ps)
        def _(n):
            ps_copy(n, te, e).wait_send()

        for h in (0, 1):
            r_copy(te, e, h).wait_send()

    for h in (0, 1):
        own_copy(partner, h).wait_send()

        @pl.loop(0, n_chip)
        def _(q):
            fw_copy(q, core, h).wait_send()
            sb_copy(q, 1 - core, h).wait_send()

    @pl.loop(1, n_y)
    def _(s):
        yy = up_y(s)
        for h in (0, 1):
            own_copy(yy * 2 + xh, h).wait_send()
        relay_y(yy).wait_send()
        relay_x(yy).wait_send()
        for x2 in range(2):
            c0_copy(yy, x2, y).wait_send()
        c1_copy(yy, y).wait_send()

    @pl.loop(0, n_y)
    def _(yy):
        x1_copy(yy).wait_send()

    x0_copy().wait_send()


def body(
    stream, queries, attn_keys, attn_values, out_weight, norm_gain, expert_ids, combine, w_gate, w_up, w_down
):
    n_ctx = lax.axis_size("ctx")
    n_exp = lax.axis_size("exp")
    span, qw = queries.shape
    toks, dim = stream.shape
    hid = w_gate.shape[2]
    heads = qw // HD
    cap = toks // 2
    slots = n_exp * cap
    n_chip = n_ctx // 2
    nt = hid // HD
    n_ps = 4
    n_y = n_ctx // 4
    w0 = dim * 3 // 8
    vm = pl.BlockSpec(memory_space=pltpu.VMEM)
    hbm = pl.BlockSpec(memory_space=pl.ANY)
    dma = pltpu.SemaphoreType.DMA
    scratch = [
        pltpu.VMEM((n_ctx, span, HD), BF),
        pltpu.VMEM((n_ctx, span, HD), BF),
        pltpu.VMEM((heads, span, HD), F32),
        pltpu.VMEM((heads, span, HD), F32),
        pltpu.VMEM((heads, span, HD), F32),
        pltpu.VMEM((span, qw), BF),
        pltpu.VMEM((qw, dim), BF),
        pltpu.VMEM((nt, dim, 2 * HD), BF),
        pltpu.VMEM((hid, dim), BF),
        pltpu.VMEM((n_ps, n_exp, toks, dim // n_ps), BF),
        pltpu.VMEM((n_ps, n_exp, toks, dim // n_ps), BF),
        pltpu.VMEM((toks, dim), F32),
        pltpu.VMEM((toks, dim), BF),
        pltpu.VMEM((n_exp, cap, dim), BF),
        pltpu.VMEM((n_exp, cap, dim), BF),
        pltpu.VMEM((n_ctx, slots, dim), BF),
        pltpu.VMEM((4 * slots, hid), BF),
        pltpu.VMEM((n_ctx, slots, dim), BF),
        pltpu.VMEM((n_chip, slots, dim), BF),
        pltpu.VMEM((n_y, 2, slots, w0), BF),
        pltpu.VMEM((n_y, slots, dim - w0), BF),
        pltpu.VMEM((n_y, slots, dim - w0), BF),
        pltpu.VMEM((slots, w0), BF),
        pltpu.VMEM((n_exp, cap, dim), BF),
        dma((3, nt)),
        dma((2, n_chip)),
        dma((2, n_ctx)),
        dma((2, n_chip)),
        dma((n_ps, n_exp)),
        dma((n_ps, n_exp)),
        dma((2, n_exp)),
        dma((2, n_exp)),
        dma((2, n_chip)),
        dma((2, n_chip)),
        dma((2, n_y)),
        dma((2, n_chip)),
        dma((2, n_chip)),
        dma((2, n_chip)),
        dma((2, n_chip)),
        dma((n_y, 2)),
        dma((n_y, 2)),
        dma((n_y,)),
        dma((n_y,)),
        dma((n_y,)),
        dma((n_y,)),
        dma((1,)),
        dma((1,)),
        dma((2, n_exp)),
        dma((2, n_exp)),
    ]
    return pl.pallas_call(
        functools.partial(layer_kernel, n_ctx, n_exp),
        out_shape=jax.ShapeDtypeStruct((toks, dim), BF),
        in_specs=[vm] * 7 + [hbm] * 4,
        out_specs=vm,
        scratch_shapes=scratch,
        compiler_params=pltpu.CompilerParams(
            collective_id=0, has_side_effects=True, vmem_limit_bytes=67_000_000
        ),
        name="decoder_layer",
    )(
        queries,
        attn_keys,
        attn_values,
        stream,
        norm_gain.reshape(1, dim),
        expert_ids.T,
        combine.T,
        out_weight,
        w_gate[0],
        w_up[0],
        w_down[0],
    )


def solution(mesh):
    in_specs = (
        P(("ctx", "exp"), None),
        P("ctx", "exp"),
        P("ctx", "exp"),
        P("ctx", "exp"),
        P("exp", None),
        P(),
        P(("ctx", "exp"), None),
        P(("ctx", "exp"), None),
        P("exp", None, "ctx"),
        P("exp", None, "ctx"),
        P("exp", "ctx", None),
    )
    out_specs = P(("ctx", "exp"), None)
    return jax.shard_map(body, mesh=mesh, in_specs=in_specs, out_specs=out_specs, check_vma=False)
```

time: 176 us -> 148 us (0.84)
  Pallas kernels: 174 us -> 146 us
    pallas_call x1, Pallas kernels: 174 us -> 146 us  [body(): pl.pallas_call(functools.partial(layer_kernel, n_ctx, n_exp), out_shape=j...]
where the time goes in v2:
time: 148 us
  Pallas kernels  146 us (99%)
  local copies, waits for them, and re-layouts  1.57 us (1%)
    pallas_call x1, Pallas kernels, body(): pl.pallas_call(functools.partial(layer_kernel, n_ctx, n_exp), out_shape=j...  146 us

profile of v2, /device:TPU:29, one launch (start us, length us, event | category | flops | bytes accessed | tf_op | source)
XLA Modules:
  0.0 147.8 jit_solution(13508098575580345497)
XLA Ops:
  0.0 146.3 %decoder_layer.1 = bf16[16,4096]{1,0:T(8,128)(2,1)} custom-call(bf16[128,512]{1,0:T(8,128)(2,1)} %q_ref.1, bf16[128,128]{1,0:T(8,128)(2,1)} %k_ref.1, bf16[128,128]{1,0:T(8,128)(2,1)} %v_ref.1, bf16[16,4096]{1,0:T(8,128)(2,1)} %stream_ref.1, f32[1,4096]{1,0:T(1,128)} %bitcast.9, s32[2,16]{1,0:T(2,128)} %bitcast.10, f32[2,16]{1,0:T(2,128)} %bitcast.11, ...), custom_call_target="tpu_custom_call" | custom-call | tf_op jit(solution)/shard_map/decoder_layer/pallas_call | solution.py:716
  146.3 1.6 %copy.13 = bf16[16,4096]{1,0:T(8,128)(2,1)} copy(bf16[16,4096]{1,0:T(8,128)(2,1)} %decoder_layer.1) | data formatting | bytes 262144

commit v3 on v2

v3 whole, which is shorter than its diff:
```python
import functools
import math

import jax
import jax.numpy as jnp
from jax import lax
from jax.experimental import pallas as pl
from jax.experimental.pallas import tpu as pltpu
from jax.sharding import PartitionSpec as P

HD = 128
MESH = pl.DeviceIdType.MESH
NEG = -1e30
F32 = jnp.float32
BF = jnp.bfloat16
NT = (((1,), (1,)), ((), ()))
TN = (((0,), (0,)), ((), ()))


def layer_kernel(
    n_ctx,
    n_exp,
    q_ref,
    k_ref,
    v_ref,
    stream_ref,
    gain_ref,
    ids_ref,
    comb_ref,
    ow_hbm,
    wg_hbm,
    wu_hbm,
    wd_hbm,
    out_ref,
    k_all,
    v_all,
    m_s,
    l_s,
    acc_s,
    att_s,
    ow_v,
    wgu_v,
    wd_v,
    ps_v,
    pr_v,
    mixed_v,
    factor_v,
    pk_v,
    a2_v,
    rows_v,
    h_v,
    part_v,
    sib_v,
    rh0_v,
    rx1_v,
    rh1_v,
    rx0_v,
    ret_v,
    w_sem,
    kv_ss,
    kv_rs,
    kf_ss,
    ps_ss,
    ps_rs,
    a_ss,
    a_rs,
    ag_ss,
    ag_rs,
    rl_ss,
    fw_ss,
    fw_rs,
    sb_ss,
    sb_rs,
    c0_ss,
    c0_rs,
    x1_ss,
    x1_rs,
    c1_ss,
    c1_rs,
    x0_ss,
    x0_rs,
    r_ss,
    r_rs,
):
    c = lax.axis_index("ctx")
    e = lax.axis_index("exp")
    span = q_ref.shape[0]
    heads = q_ref.shape[1] // HD
    toks, dim = stream_ref.shape
    cap = pk_v.shape[1]
    slots = n_exp * cap
    n_chip = n_ctx // 2
    core = lax.rem(c, 2)
    chip = c // 2
    y = c // 4
    xh = lax.rem(chip, 2)
    partner = chip + 1 - 2 * xh
    sibling = chip * 2 + 1 - core
    n_y = n_ctx // 4
    nt = wgu_v.shape[0]
    n_ps = ps_v.shape[0]
    n_p = n_ps
    pw = dim // n_p
    w0 = rh0_v.shape[3] // n_p
    w1 = pw - w0
    g0 = pw * 3 // 8
    far = rows_v.shape[2] - dim

    def extra(p):
        return far if p == n_p - 1 else 0

    def whole_cols(p):
        return pl.ds(p * pw, pw)

    def sent_cols(p):
        return pl.ds(p * pw, pw + extra(p))

    def route_cols(p, h):
        return pl.ds(p * pw, w1) if h else pl.ds(p * pw + w1, w0)

    def sent_route_cols(p, h):
        return pl.ds(p * pw, pw - g0) if h else pl.ds(p * pw + pw - g0, g0 + extra(p))

    def near(p, h):
        return pl.ds(p * w1, w1) if h else pl.ds(p * w0, w0)

    def remote(src, dst, ss, rs, tc, te):
        return pltpu.make_async_remote_copy(
            src_ref=src, dst_ref=dst, send_sem=ss, recv_sem=rs, device_id=(tc, te), device_id_type=MESH
        )

    def weight_copies(n):
        cols = pl.ds(pl.multiple_of(n * HD, HD), HD)
        return (
            pltpu.make_async_copy(wg_hbm.at[:, cols], wgu_v.at[n, :, pl.ds(0, HD)], w_sem.at[0, n]),
            pltpu.make_async_copy(wu_hbm.at[:, cols], wgu_v.at[n, :, pl.ds(HD, HD)], w_sem.at[1, n]),
        )

    ow_copy = pltpu.make_async_copy(ow_hbm, ow_v, w_sem.at[2, 0])
    wd_copy = pltpu.make_async_copy(wd_hbm, wd_v, w_sem.at[2, 1])
    ow_copy.start()

    barrier = pltpu.get_barrier_semaphore()
    pl.semaphore_signal(barrier, inc=1, device_id=(sibling, e), device_id_type=MESH)

    @pl.loop(1, n_chip)
    def _(d):
        tc = lax.rem(chip + d, n_chip) * 2 + core
        pl.semaphore_signal(barrier, inc=1, device_id=(tc, e), device_id_type=MESH)

    @pl.loop(1, n_exp)
    def _(d):
        pl.semaphore_signal(barrier, inc=1, device_id=(c, lax.rem(e + d, n_exp)), device_id_type=MESH)

    pl.semaphore_wait(barrier, n_chip + n_exp - 1)

    def kv_pair(to_chip, block):
        return (
            remote(k_ref, k_all.at[block], kv_ss.at[0, to_chip], kv_rs.at[0, block], to_chip * 2 + core, e),
            remote(v_ref, v_all.at[block], kv_ss.at[1, to_chip], kv_rs.at[1, block], to_chip * 2 + core, e),
        )

    def kv_own():
        return (
            remote(k_ref, k_all.at[c], kf_ss.at[0, chip], kv_rs.at[0, c], sibling, e),
            remote(v_ref, v_all.at[c], kf_ss.at[1, chip], kv_rs.at[1, c], sibling, e),
        )

    def kv_forward(q):
        b = q * 2 + core
        return (
            remote(k_all.at[b], k_all.at[b], kf_ss.at[0, q], kv_rs.at[0, b], sibling, e),
            remote(v_all.at[b], v_all.at[b], kf_ss.at[1, q], kv_rs.at[1, b], sibling, e),
        )

    @pl.when(core == 0)
    def _():
        for cp in kv_own():
            cp.start()

    @pl.loop(chip + 1, n_chip)
    def _(q):
        for cp in kv_pair(q, c):
            cp.start()

    @pl.loop(0, nt)
    def _(n):
        for cp in weight_copies(n):
            cp.start()

    wd_copy.start()

    k_all[c] = k_ref[...]
    v_all[c] = v_ref[...]

    @pl.loop(c + 1, y * 4 + 4)
    def _(j):
        k_all[j] = jnp.zeros(k_ref.shape, BF)
        v_all[j] = jnp.zeros(v_ref.shape, BF)

    m_s[...] = jnp.full(m_s.shape, NEG, F32)
    l_s[...] = jnp.zeros(l_s.shape, F32)
    acc_s[...] = jnp.zeros(acc_s.shape, F32)
    scale = 1.0 / math.sqrt(HD)

    def step_off(s):
        return s ^ (s // 2)

    def forward_group(g):
        @pl.loop(g * 2, jnp.minimum(g * 2 + 2, chip))
        def _(q):
            for cp in kv_pair(chip, q * 2 + core):
                cp.wait_recv()
            for cp in kv_forward(q):
                cp.start()

    forward_group(y)

    @pl.loop(0, n_y)
    def _(s):
        g = y - step_off(s)
        g2 = y - step_off(s + 1)

        @pl.when((s < n_y - 1) & (g2 >= 0))
        def _():
            forward_group(g2)

        @pl.when(g >= 0)
        def _():
            @pl.loop(g * 2, jnp.minimum(g * 2 + 2, (c + core) // 2))
            def _(q):
                for cp in kv_pair(chip, q * 2 + 1 - core):
                    cp.wait_recv()

            keys = k_all[pl.ds(g * 4, 4)].reshape(4 * span, HD)
            vals = v_all[pl.ds(g * 4, 4)].reshape(4 * span, HD)
            row = lax.broadcasted_iota(jnp.int32, (span, 4 * span), 0) + (c - g * 4) * span
            col = lax.broadcasted_iota(jnp.int32, (span, 4 * span), 1)
            allowed = row >= col
            for h in range(heads):
                q_h = q_ref[:, h * HD : (h + 1) * HD]
                s_h = lax.dot_general(q_h, keys, NT, preferred_element_type=F32) * scale
                s_h = jnp.where(allowed, s_h, NEG)
                m_old = m_s[h]
                m_new = jnp.maximum(m_old, jnp.max(s_h, axis=1, keepdims=True))
                p = jnp.exp(s_h - m_new[:, :1])
                fix = jnp.exp(m_old - m_new)
                l_s[h] = l_s[h] * fix + jnp.sum(p, axis=1, keepdims=True)
                acc_s[h] = acc_s[h] * fix + jnp.dot(p.astype(BF), vals, preferred_element_type=F32)
                m_s[h] = m_new

    for h in range(heads):
        att_s[:, h * HD : (h + 1) * HD] = (acc_s[h] / l_s[h]).astype(BF)

    ow_copy.wait()

    def ps_copy(n, te, src_e):
        return remote(ps_v.at[n, te], pr_v.at[n, src_e], ps_ss.at[n, te], ps_rs.at[n, src_e], c, te)

    def project(n):
        r = jnp.dot(att_s[...], ow_v[:, whole_cols(n)], preferred_element_type=F32)
        ps_v[n] = r.reshape(n_exp, toks, pw).astype(BF)

        @pl.loop(1, n_exp)
        def _(d):
            ps_copy(n, lax.rem(e + d, n_exp), e).start()

        pr_v[n, e] = ps_v[n, e]

    project(0)
    project(1)

    slot_row = lax.broadcasted_iota(jnp.int32, (slots, toks), 0)
    slot_exp = slot_row // cap
    first = ids_ref[0:1, :] == slot_exp
    second = ids_ref[1:2, :] == slot_exp
    named = jnp.where(first | second, 1.0, 0.0)
    tri = jnp.where(
        lax.broadcasted_iota(jnp.int32, (toks, toks), 0) < lax.broadcasted_iota(jnp.int32, (toks, toks), 1), 1.0, 0.0
    )
    rank = jnp.dot(named.astype(BF), tri.astype(BF), preferred_element_type=F32)
    slot_rank = (slot_row - slot_exp * cap).astype(F32)
    chosen = jnp.where(rank == slot_rank, named, 0.0)
    chosen_bf = chosen.astype(BF)

    def a_copy(te, src_e, p):
        cols = sent_cols(p)
        return remote(pk_v.at[te, :, cols], a2_v.at[src_e, :, cols], a_ss.at[p, te], a_rs.at[p, src_e], c, te)

    def picked(values):
        r = jnp.dot(chosen_bf, values, preferred_element_type=F32)
        return r.reshape(n_exp, cap, values.shape[1]).astype(BF)

    def dispatch(p, square_sum):
        @pl.loop(1, n_exp)
        def _(d):
            ps_copy(p, e, lax.rem(e + d, n_exp)).wait_recv()

        cols = whole_cols(p)
        mixed = stream_ref[:, cols].astype(F32) + jnp.sum(pr_v[p].astype(F32), axis=0)
        mixed_v[:, cols] = mixed
        square_sum = square_sum + jnp.sum(mixed * mixed, axis=1, keepdims=True)
        pk_v[:, :, cols] = picked((mixed * gain_ref[:, cols]).astype(BF))
        if p == n_p - 1:
            factor = lax.rsqrt(square_sum / dim + 1e-05)
            high = factor.astype(BF).astype(F32)
            middle = (factor - high).astype(BF).astype(F32)
            low = factor - high - middle
            lane = lax.broadcasted_iota(jnp.int32, (toks, far), 1)
            terms = jnp.where(lane == 0, high, jnp.where(lane == 1, middle, jnp.where(lane == 2, low, 0.0)))
            pk_v[:, :, dim : dim + far] = picked(terms.astype(BF))

        @pl.loop(1, n_exp)
        def _(d):
            a_copy(lax.rem(e + d, n_exp), e, p).start()

        a2_v[e, :, sent_cols(p)] = pk_v[e, :, sent_cols(p)]
        return square_sum

    def row_copy(to_chip, q, p, cols, ss, rs):
        part = rows_v.at[q * 2 + core, :, cols]
        return remote(part, part, ss, rs, to_chip * 2 + core, e)

    def own_copy(to_chip, p):
        return row_copy(to_chip, chip, p, sent_cols(p), ag_ss.at[p, to_chip], ag_rs.at[0, p, chip])

    def arrived(q, p):
        row_copy(chip, q, p, sent_cols(p), ag_ss.at[p, chip], ag_rs.at[0, p, q]).wait_recv()

    def arrived_route(q, p, h):
        row_copy(chip, q, p, sent_route_cols(p, h), ag_ss.at[p, chip], ag_rs.at[h, p, q]).wait_recv()

    def relay_y(ty, p):
        return row_copy(ty * 2 + xh, partner, p, sent_route_cols(p, 0), rl_ss.at[0, p, ty], ag_rs.at[0, p, partner])

    def relay_x(yy, p):
        q = yy * 2 + xh
        return row_copy(partner, q, p, sent_route_cols(p, 1), rl_ss.at[1, p, yy], ag_rs.at[1, p, q])

    def fw_copy(q, of_core, p):
        part = rows_v.at[q * 2 + of_core, :, sent_cols(p)]
        return remote(part, part, fw_ss.at[p, q], fw_rs.at[p, q], sibling, e)

    def row_off(s):
        return lax.rem(s, 2) * 2 + s // 2

    def down_y(s):
        return lax.rem(y + n_y - row_off(s), n_y)

    def up_y(s):
        return lax.rem(y + row_off(s), n_y)

    def spread(p):
        @pl.loop(1, n_exp)
        def _(d):
            a_copy(e, lax.rem(e + d, n_exp), p).wait_recv()

        cols = sent_cols(p)
        rows_v[c, :, cols] = a2_v[:, :, cols].astype(F32).reshape(slots, pw + extra(p)).astype(BF)
        own_copy(partner, p).start()

        @pl.loop(1, n_y)
        def _(s):
            own_copy(down_y(s) * 2 + xh, p).start()

        fw_copy(chip, core, p).start()

    def partner_rows(p):
        arrived(partner, p)

        @pl.loop(1, n_y)
        def _(s):
            relay_y(down_y(s), p).start()

        fw_copy(partner, core, p).start()

    def column_rows(s, p):
        q = up_y(s) * 2 + xh
        arrived(q, p)
        relay_x(up_y(s), p).start()
        fw_copy(q, core, p).start()

    def near_rows(p):
        partner_rows(p)

        @pl.loop(1, n_y - 1)
        def _(s):
            column_rows(s, p)

    def other_rows(s, p):
        q = up_y(s) * 2 + 1 - xh
        for h in (0, 1):
            arrived_route(q, p, h)
        fw_copy(q, core, p).start()

    square_sum = jnp.zeros((toks, 1), F32)
    for p in range(n_p):
        square_sum = dispatch(p, square_sum)
        if p + 2 < n_p:
            project(p + 2)
        if p >= 1:
            spread(p - 1)
        if p >= 2:
            near_rows(p - 2)
    spread(n_p - 1)
    near_rows(n_p - 2)
    near_rows(n_p - 1)
    for p in range(n_p - 1):
        column_rows(n_y - 1, p)

    @pl.loop(0, nt)
    def _(n):
        for cp in weight_copies(n):
            cp.wait()

    wd_copy.wait()

    def sb_copy(q, of_core, p):
        cols = whole_cols(p)
        return remote(
            part_v.at[q * 2 + of_core, :, cols], sib_v.at[q, :, cols], sb_ss.at[p, q], sb_rs.at[p, q], sibling, e
        )

    def c0_copy(yy, x2, src_y, p):
        return remote(
            part_v.at[(yy * 2 + x2) * 2 + core, :, route_cols(p, 0)],
            rh0_v.at[src_y, x2, :, near(p, 0)],
            c0_ss.at[p, yy, x2],
            c0_rs.at[p, src_y, x2],
            (yy * 2 + xh) * 2 + core,
            e,
        )

    def x1_copy(yy, p):
        return remote(
            part_v.at[(yy * 2 + 1 - xh) * 2 + core, :, route_cols(p, 1)],
            rx1_v.at[yy, :, near(p, 1)],
            x1_ss.at[p, yy],
            x1_rs.at[p, yy],
            partner * 2 + core,
            e,
        )

    def c1_copy(yy, src_y, p):
        b = (yy * 2 + xh) * 2 + core
        return remote(
            part_v.at[b, :, route_cols(p, 1)],
            rh1_v.at[src_y, :, near(p, 1)],
            c1_ss.at[p, yy],
            c1_rs.at[p, src_y],
            b,
            e,
        )

    def x0_copy(p):
        b = partner * 2 + core
        return remote(
            part_v.at[b, :, route_cols(p, 0)], rx0_v.at[:, near(p, 0)], x0_ss.at[p], x0_rs.at[p], b, e
        )

    def over_cores(yy, p):
        cols = whole_cols(p)
        for x2 in range(2):
            q = yy * 2 + x2
            b = q * 2 + core
            sb_copy(q, core, p).wait_recv()
            part_v[b, :, cols] = (part_v[b, :, cols].astype(F32) + sib_v[q, :, cols].astype(F32)).astype(BF)
        x1_copy(yy, p).start()

        @pl.when(yy != y)
        def _():
            for x2 in range(2):
                c0_copy(yy, x2, y, p).start()

    def over_x(yy, p):
        x1_copy(yy, p).wait_recv()
        b = (yy * 2 + xh) * 2 + core
        cols = route_cols(p, 1)
        part_v[b, :, cols] = (part_v[b, :, cols].astype(F32) + rx1_v[yy, :, near(p, 1)].astype(F32)).astype(BF)

        @pl.when(yy != y)
        def _():
            c1_copy(yy, y, p).start()

    rows_chunk = 4 * slots

    @pl.loop(0, n_y)
    def _(s):
        yy = up_y(s)

        @pl.when(s == 1)
        def _():
            for p in range(n_p):
                other_rows(1, p)

        for x2 in range(2):
            for p in range(n_p):
                fw_copy(yy * 2 + x2, 1 - core, p).wait_recv()

        terms = rows_v[pl.ds(yy * 4, 4), :, dim : dim + far].reshape(rows_chunk, far).astype(F32)
        factor_v[...] = jnp.broadcast_to(jnp.sum(terms, axis=1, keepdims=True), (rows_chunk, HD))

        @pl.loop(0, nt)
        def _(n):
            x = rows_v[pl.ds(yy * 4, 4), :, 0:dim].reshape(rows_chunk, dim)
            r = jnp.dot(x, wgu_v[n], preferred_element_type=F32)
            g = r[:, :HD] * factor_v[...]
            u = r[:, HD:] * factor_v[...]
            h_v[:, pl.ds(pl.multiple_of(n * HD, HD), HD)] = (g / (1.0 + jnp.exp(-g)) * u).astype(BF)

        @pl.when(s == 0)
        def _():
            column_rows(n_y - 1, n_p - 1)

        @pl.when((s > 0) & (s < n_y - 1))
        def _():
            for p in range(n_p):
                other_rows(s + 1, p)

        @pl.when(s > 0)
        def _():
            for p in range(n_p):
                over_cores(up_y(s - 1), p)

        @pl.when(s > 1)
        def _():
            for p in range(n_p):
                over_x(up_y(s - 2), p)

        for p in range(n_p):
            o = jnp.dot(h_v[...], wd_v[:, whole_cols(p)], preferred_element_type=F32)
            part_v[pl.ds(yy * 4, 4), :, whole_cols(p)] = o.astype(BF).reshape(4, slots, pw)
            for x2 in range(2):
                sb_copy(yy * 2 + x2, 1 - core, p).start()

    for p in range(n_p):
        over_cores(up_y(n_y - 1), p)
    for p in range(n_p):
        over_x(up_y(n_y - 2), p)
    for p in range(n_p):
        over_x(up_y(n_y - 1), p)

    def column_sum(b, x2, p):
        total = part_v[b, :, route_cols(p, 0)].astype(F32)
        for d in range(1, n_y):
            total = total + rh0_v[lax.rem(y + d, n_y), x2, :, near(p, 0)].astype(F32)
        return total

    for p in range(n_p):

        @pl.loop(1, n_y)
        def _(d):
            for x2 in range(2):
                c0_copy(y, x2, lax.rem(y + d, n_y), p).wait_recv()

        b = partner * 2 + core
        part_v[b, :, route_cols(p, 0)] = column_sum(b, 1 - xh, p).astype(BF)
        x0_copy(p).start()

    def r_copy(te, src_e, p):
        cols = whole_cols(p)
        return remote(pk_v.at[te, :, cols], ret_v.at[src_e, :, cols], r_ss.at[p, te], r_rs.at[p, src_e], c, te)

    for p in range(n_p):

        @pl.loop(1, n_exp)
        def _(d):
            a_copy(lax.rem(e + d, n_exp), e, p).wait_send()

        @pl.loop(1, n_y)
        def _(d):
            c1_copy(y, lax.rem(y + d, n_y), p).wait_recv()

        total = part_v[c, :, route_cols(p, 1)].astype(F32)
        for d in range(1, n_y):
            total = total + rh1_v[lax.rem(y + d, n_y), :, near(p, 1)].astype(F32)
        pk_v[:, :, route_cols(p, 1)] = total.reshape(n_exp, cap, w1).astype(BF)
        x0_copy(p).wait_recv()
        total = column_sum(c, xh, p) + rx0_v[:, near(p, 0)].astype(F32)
        pk_v[:, :, route_cols(p, 0)] = total.reshape(n_exp, cap, w0).astype(BF)

        @pl.loop(1, n_exp)
        def _(d):
            r_copy(lax.rem(e + d, n_exp), e, p).start()

        ret_v[e, :, whole_cols(p)] = pk_v[e, :, whole_cols(p)]

    wt = chosen * jnp.where(first, comb_ref[0:1, :], comb_ref[1:2, :])
    w_hi = wt.astype(BF)
    w_lo = (wt - w_hi.astype(F32)).astype(BF)

    for p in range(n_p):

        @pl.loop(1, n_exp)
        def _(d):
            r_copy(e, lax.rem(e + d, n_exp), p).wait_recv()

        cols = whole_cols(p)
        r = ret_v[:, :, cols].astype(F32).reshape(slots, pw).astype(BF)
        o = lax.dot_general(w_hi, r, TN, preferred_element_type=F32)
        o = o + lax.dot_general(w_lo, r, TN, preferred_element_type=F32)
        out_ref[:, cols] = (mixed_v[:, cols] + o).astype(BF)

    @pl.when(core == 0)
    def _():
        for cp in kv_own():
            cp.wait_send()

    @pl.loop(chip + 1, n_chip)
    def _(q):
        for cp in kv_pair(q, c):
            cp.wait_send()

    @pl.loop(0, chip)
    def _(q):
        for cp in kv_forward(q):
            cp.wait_send()

    for p in range(n_p):

        @pl.loop(1, n_exp)
        def _(d):
            te = lax.rem(e + d, n_exp)
            ps_copy(p, te, e).wait_send()
            r_copy(te, e, p).wait_send()

        own_copy(partner, p).wait_send()
        x0_copy(p).wait_send()

        @pl.loop(0, n_chip)
        def _(q):
            fw_copy(q, core, p).wait_send()
            sb_copy(q, 1 - core, p).wait_send()

        @pl.loop(1, n_y)
        def _(s):
            yy = up_y(s)
            own_copy(yy * 2 + xh, p).wait_send()
            relay_y(yy, p).wait_send()
            relay_x(yy, p).wait_send()
            for x2 in range(2):
                c0_copy(yy, x2, y, p).wait_send()
            c1_copy(yy, y, p).wait_send()

        @pl.loop(0, n_y)
        def _(yy):
            x1_copy(yy, p).wait_send()


def body(
    stream, queries, attn_keys, attn_values, out_weight, norm_gain, expert_ids, combine, w_gate, w_up, w_down
):
    n_ctx = lax.axis_size("ctx")
    n_exp = lax.axis_size("exp")
    span, qw = queries.shape
    toks, dim = stream.shape
    hid = w_gate.shape[2]
    heads = qw // HD
    cap = toks // 2
    slots = n_exp * cap
    n_chip = n_ctx // 2
    nt = hid // HD
    n_ps = 4
    n_y = n_ctx // 4
    w0 = dim * 3 // 8
    vm = pl.BlockSpec(memory_space=pltpu.VMEM)
    hbm = pl.BlockSpec(memory_space=pl.ANY)
    dma = pltpu.SemaphoreType.DMA
    scratch = [
        pltpu.VMEM((n_ctx, span, HD), BF),
        pltpu.VMEM((n_ctx, span, HD), BF),
        pltpu.VMEM((heads, span, HD), F32),
        pltpu.VMEM((heads, span, HD), F32),
        pltpu.VMEM((heads, span, HD), F32),
        pltpu.VMEM((span, qw), BF),
        pltpu.VMEM((qw, dim), BF),
        pltpu.VMEM((nt, dim, 2 * HD), BF),
        pltpu.VMEM((hid, dim), BF),
        pltpu.VMEM((n_ps, n_exp, toks, dim // n_ps), BF),
        pltpu.VMEM((n_ps, n_exp, toks, dim // n_ps), BF),
        pltpu.VMEM((toks, dim), F32),
        pltpu.VMEM((4 * slots, HD), F32),
        pltpu.VMEM((n_exp, cap, dim + HD), BF),
        pltpu.VMEM((n_exp, cap, dim + HD), BF),
        pltpu.VMEM((n_ctx, slots, dim + HD), BF),
        pltpu.VMEM((4 * slots, hid), BF),
        pltpu.VMEM((n_ctx, slots, dim), BF),
        pltpu.VMEM((n_chip, slots, dim), BF),
        pltpu.VMEM((n_y, 2, slots, w0), BF),
        pltpu.VMEM((n_y, slots, dim - w0), BF),
        pltpu.VMEM((n_y, slots, dim - w0), BF),
        pltpu.VMEM((slots, w0), BF),
        pltpu.VMEM((n_exp, cap, dim), BF),
        dma((3, nt)),
        dma((2, n_chip)),
        dma((2, n_ctx)),
        dma((2, n_chip)),
        dma((n_ps, n_exp)),
        dma((n_ps, n_exp)),
        dma((n_ps, n_exp)),
        dma((n_ps, n_exp)),
        dma((n_ps, n_chip)),
        dma((2, n_ps, n_chip)),
        dma((2, n_ps, n_y)),
        dma((n_ps, n_chip)),
        dma((n_ps, n_chip)),
        dma((n_ps, n_chip)),
        dma((n_ps, n_chip)),
        dma((n_ps, n_y, 2)),
        dma((n_ps, n_y, 2)),
        dma((n_ps, n_y)),
        dma((n_ps, n_y)),
        dma((n_ps, n_y)),
        dma((n_ps, n_y)),
        dma((n_ps,)),
        dma((n_ps,)),
        dma((n_ps, n_exp)),
        dma((n_ps, n_exp)),
    ]
    return pl.pallas_call(
        functools.partial(layer_kernel, n_ctx, n_exp),
        out_shape=jax.ShapeDtypeStruct((toks, dim), BF),
        in_specs=[vm] * 7 + [hbm] * 4,
        out_specs=vm,
        scratch_shapes=scratch,
        compiler_params=pltpu.CompilerParams(
            collective_id=0, has_side_effects=True, vmem_limit_bytes=67_000_000
        ),
        name="decoder_layer",
    )(
        queries,
        attn_keys,
        attn_values,
        stream,
        norm_gain.reshape(1, dim),
        expert_ids.T,
        combine.T,
        out_weight,
        w_gate[0],
        w_up[0],
        w_down[0],
    )


def solution(mesh):
    in_specs = (
        P(("ctx", "exp"), None),
        P("ctx", "exp"),
        P("ctx", "exp"),
        P("ctx", "exp"),
        P("exp", None),
        P(),
        P(("ctx", "exp"), None),
        P(("ctx", "exp"), None),
        P("exp", None, "ctx"),
        P("exp", None, "ctx"),
        P("exp", "ctx", None),
    )
    out_specs = P(("ctx", "exp"), None)
    return jax.shard_map(body, mesh=mesh, in_specs=in_specs, out_specs=out_specs, check_vma=False)
```

time: 148 us -> 136 us (0.919); the launches traced: 148 us -> 134 us
  Pallas kernels: 146 us -> 132 us
    pallas_call x1, Pallas kernels: 146 us -> 132 us  [body(): pl.pallas_call(functools.partial(layer_kernel, n_ctx, n_exp), out_shape=j...]
where the time goes in v3:
time: 136 us; the launch traced here: 134 us
  Pallas kernels  132 us (97%)
  local copies, waits for them, and re-layouts  1.57 us (1%)
    pallas_call x1, Pallas kernels, body(): pl.pallas_call(functools.partial(layer_kernel, n_ctx, n_exp), out_shape=j...  132 us

profile of v3, /device:TPU:29, one launch (start us, length us, event | category | flops | bytes accessed | tf_op | source)
XLA Modules:
  0.0 133.5 jit_solution(153899990869979220)
XLA Ops:
  0.0 131.9 %decoder_layer.1 = bf16[16,4096]{1,0:T(8,128)(2,1)} custom-call(bf16[128,512]{1,0:T(8,128)(2,1)} %q_ref.1, bf16[128,128]{1,0:T(8,128)(2,1)} %k_ref.1, bf16[128,128]{1,0:T(8,128)(2,1)} %v_ref.1, bf16[16,4096]{1,0:T(8,128)(2,1)} %stream_ref.1, f32[1,4096]{1,0:T(1,128)} %bitcast.9, s32[2,16]{1,0:T(2,128)} %bitcast.10, f32[2,16]{1,0:T(2,128)} %bitcast.11, ...), custom_call_target="tpu_custom_call" | custom-call | tf_op jit(solution)/shard_map/decoder_layer/pallas_call | solution.py:720
  131.9 1.6 %copy.13 = bf16[16,4096]{1,0:T(8,128)(2,1)} copy(bf16[16,4096]{1,0:T(8,128)(2,1)} %decoder_layer.1) | data formatting | bytes 262144

commit v4 on v3

--- a/solution.py
+++ b/solution.py
@@ -488,6 +488,11 @@
     def _(s):
         yy = up_y(s)
 
+        @pl.when(s > 0)
+        def _():
+            for p in range(n_p):
+                over_cores(up_y(s - 1), p)
+
         @pl.when(s == 1)
         def _():
             for p in range(n_p):
@@ -517,21 +522,16 @@
             for p in range(n_p):
                 other_rows(s + 1, p)
 
-        @pl.when(s > 0)
-        def _():
-            for p in range(n_p):
-                over_cores(up_y(s - 1), p)
-
-        @pl.when(s > 1)
-        def _():
-            for p in range(n_p):
-                over_x(up_y(s - 2), p)
-
         for p in range(n_p):
             o = jnp.dot(h_v[...], wd_v[:, whole_cols(p)], preferred_element_type=F32)
             part_v[pl.ds(yy * 4, 4), :, whole_cols(p)] = o.astype(BF).reshape(4, slots, pw)
             for x2 in range(2):
                 sb_copy(yy * 2 + x2, 1 - core, p).start()
+
+        @pl.when((s > 0) & (s < n_y - 1))
+        def _():
+            for p in range(n_p):
+                over_x(up_y(s - 1), p)
 
     for p in range(n_p):
         over_cores(up_y(n_y - 1), p)

time: 136 us -> 133 us (0.978)
  Pallas kernels: 132 us -> 129 us
    pallas_call x1, Pallas kernels: 132 us -> 129 us  [body(): pl.pallas_call(functools.partial(layer_kernel, n_ctx, n_exp), out_shape=j...]
where the time goes in v4:
time: 133 us; the launch traced here: 131 us
  Pallas kernels  129 us (97%)
  local copies, waits for them, and re-layouts  1.57 us (1%)
    pallas_call x1, Pallas kernels, body(): pl.pallas_call(functools.partial(layer_kernel, n_ctx, n_exp), out_shape=j...  129 us

profile of v4, /device:TPU:29, one launch (start us, length us, event | category | flops | bytes accessed | tf_op | source)
XLA Modules:
  0.0 130.9 jit_solution(7784240797046230329)
XLA Ops:
  0.0 129.3 %decoder_layer.1 = bf16[16,4096]{1,0:T(8,128)(2,1)} custom-call(bf16[128,512]{1,0:T(8,128)(2,1)} %q_ref.1, bf16[128,128]{1,0:T(8,128)(2,1)} %k_ref.1, bf16[128,128]{1,0:T(8,128)(2,1)} %v_ref.1, bf16[16,4096]{1,0:T(8,128)(2,1)} %stream_ref.1, f32[1,4096]{1,0:T(1,128)} %bitcast.9, s32[2,16]{1,0:T(2,128)} %bitcast.10, f32[2,16]{1,0:T(2,128)} %bitcast.11, ...), custom_call_target="tpu_custom_call" | custom-call | tf_op jit(solution)/shard_map/decoder_layer/pallas_call | solution.py:720
  129.3 1.6 %copy.13 = bf16[16,4096]{1,0:T(8,128)(2,1)} copy(bf16[16,4096]{1,0:T(8,128)(2,1)} %decoder_layer.1) | data formatting | bytes 262144

commit v5 on v4

--- a/solution.py
+++ b/solution.py
@@ -104,6 +104,7 @@
     w0 = rh0_v.shape[3] // n_p
     w1 = pw - w0
     g0 = pw * 3 // 8
+    g0 = pw * 3 // 8
     far = rows_v.shape[2] - dim
 
     def extra(p):
@@ -182,13 +183,6 @@
     def _(q):
         for cp in kv_pair(q, c):
             cp.start()
-
-    @pl.loop(0, nt)
-    def _(n):
-        for cp in weight_copies(n):
-            cp.start()
-
-    wd_copy.start()
 
     k_all[c] = k_ref[...]
     v_all[c] = v_ref[...]
@@ -254,6 +248,13 @@
 
     ow_copy.wait()
 
+    @pl.loop(0, nt)
+    def _(n):
+        for cp in weight_copies(n):
+            cp.start()
+
+    wd_copy.start()
+
     def ps_copy(n, te, src_e):
         return remote(ps_v.at[n, te], pr_v.at[n, src_e], ps_ss.at[n, te], ps_rs.at[n, src_e], c, te)
 
@@ -535,7 +536,6 @@
 
     for p in range(n_p):
         over_cores(up_y(n_y - 1), p)
-    for p in range(n_p):
         over_x(up_y(n_y - 2), p)
     for p in range(n_p):
         over_x(up_y(n_y - 1), p)
@@ -662,7 +662,7 @@
     nt = hid // HD
     n_ps = 4
     n_y = n_ctx // 4
-    w0 = dim * 3 // 8
+    w0 = dim * 2 // 8
     vm = pl.BlockSpec(memory_space=pltpu.VMEM)
     hbm = pl.BlockSpec(memory_space=pl.ANY)
     dma = pltpu.SemaphoreType.DMA

time: 133 us -> 134 us (level)
  the two profiles are of different devices: /device:TPU:29 before, /device:TPU:18 now
where the time goes in v5:
time: 134 us
  Pallas kernels  132 us (99%)
  local copies, waits for them, and re-layouts  1.57 us (1%)
    pallas_call x1, Pallas kernels, body(): pl.pallas_call(functools.partial(layer_kernel, n_ctx, n_exp), out_shape=j...  132 us

profile of v5, /device:TPU:18, one launch (start us, length us, event | category | flops | bytes accessed | tf_op | source)
XLA Modules:
  0.0 133.6 jit_solution(3188343256989351513)
XLA Ops:
  0.0 132.0 %decoder_layer.1 = bf16[16,4096]{1,0:T(8,128)(2,1)} custom-call(bf16[128,512]{1,0:T(8,128)(2,1)} %q_ref.1, bf16[128,128]{1,0:T(8,128)(2,1)} %k_ref.1, bf16[128,128]{1,0:T(8,128)(2,1)} %v_ref.1, bf16[16,4096]{1,0:T(8,128)(2,1)} %stream_ref.1, f32[1,4096]{1,0:T(1,128)} %bitcast.9, s32[2,16]{1,0:T(2,128)} %bitcast.10, f32[2,16]{1,0:T(2,128)} %bitcast.11, ...), custom_call_target="tpu_custom_call" | custom-call | tf_op jit(solution)/shard_map/decoder_layer/pallas_call | solution.py:720
  132.0 1.6 %copy.13 = bf16[16,4096]{1,0:T(8,128)(2,1)} copy(bf16[16,4096]{1,0:T(8,128)(2,1)} %decoder_layer.1) | data formatting | bytes 262144
